TPU v7x, 32 devices: a whole 2x2x4 slice. The times are simulated.
32 devices in a mesh: dp: 8 (over z, x), seq: 4 (over y, core).
Axes of the slice: x: 2, y: 2, z: 4, core: 2. Of those that a mesh axis runs over, the one named last changes fastest.
Arguments:
- caption_tokens: bfloat16 [128, 128, 768], P(('dp', 'seq')), may hold values from -6 to 6
- image_tokens: bfloat16 [128, 196, 768], P(('dp', 'seq')), may hold values from -6 to 6
- caption_lengths: int32 [128], P(('dp', 'seq')), may hold values from 8 to 128, as said below
- caption_image: int32 [128], P('dp'), may hold values from 0 to 127, as said below
- norm_gain: bfloat16 [768, 3], P(('dp', 'seq')), may hold values from 0.099609375 to 1.8984375
- norm_bias: bfloat16 [768, 3], P(('dp', 'seq')), may hold values from -1.25 to 1.25
- self_packed: bfloat16 [768, 2304], P(('dp', 'seq')), may hold values from -0.21875 to 0.21875
- self_output: bfloat16 [768, 768], P(('dp', 'seq')), may hold values from -0.625 to 0.625
- cross_query: bfloat16 [768, 768], P(('dp', 'seq')), may hold values from -0.21875 to 0.21875
- cross_pair: bfloat16 [768, 1536], P(('dp', 'seq')), may hold values from -0.21875 to 0.21875
- cross_output: bfloat16 [768, 768], P(('dp', 'seq')), may hold values from -0.75 to 0.75
- expand_weight: bfloat16 [768, 3072], P(('dp', 'seq')), may hold values from -0.21875 to 0.21875
- reduce_weight: bfloat16 [3072, 768], P(('dp', 'seq')), may hold values from -0.109375 to 0.109375
- cotangent: bfloat16 [128, 128, 768], P(('dp', 'seq')), may hold values from -6 to 6
Outputs:
- caption_out: bfloat16 [128, 128, 768], P(('dp', 'seq'))
- caption_grad: bfloat16 [128, 128, 768], P(('dp', 'seq'))
- image_grad: bfloat16 [128, 196, 768], P(('dp', 'seq'))
- gain_grad: float32 [768, 3], P(('dp', 'seq'))
- bias_grad: float32 [768, 3], P(('dp', 'seq'))
- self_packed_grad: float32 [768, 2304], P(('dp', 'seq'))
- self_output_grad: float32 [768, 768], P(('dp', 'seq'))
- cross_query_grad: float32 [768, 768], P(('dp', 'seq'))
- cross_pair_grad: float32 [768, 1536], P(('dp', 'seq'))
- cross_output_grad: float32 [768, 768], P(('dp', 'seq'))
- expand_grad: float32 [768, 3072], P(('dp', 'seq'))
- reduce_grad: float32 [3072, 768], P(('dp', 'seq'))
Inputs may be any that keep to these rules, and one draw needn't show every extreme that they name: `caption_lengths`: each aligned block of 4 captions holds at least one caption of length 128. `caption_image`: A permutation of the image indices. Caption c and its image lie in the same aligned block of 16; of each aligned block of 4 captions exactly 1 has its image in each aligned block of 4 images of that group.
All inputs are finite; a program needn't handle non-finite values.
Results may differ from a plain program's by a relative error of at most 0.022.
Values may be sent and summed in bfloat16 or wider, within the bound.
No kernel may reach another device: no remote copies, remote signals or barrier semaphores. Data moves between devices by JAX's collectives and lax.ppermute only.
A program may use at most 192 MiB of HBM per device.

v0:
```python
import math

import jax
import jax.numpy as jnp
from jax import lax
from jax.sharding import PartitionSpec as P

HEADS = 12
HEAD_DIM = 64


epsilon = 1e-05


def split_heads(values):
    return values.reshape(values.shape[:-1] + (HEADS, HEAD_DIM))


def project(values, weight):
    flat_rows = values.reshape(-1, values.shape[-1])
    return jnp.dot(flat_rows, weight, preferred_element_type=jnp.float32).reshape(
        values.shape[:-1] + (weight.shape[1],)
    )


def project_back(values, weight):
    flat_rows = values.reshape(-1, values.shape[-1])
    result = lax.dot_general(
        flat_rows, weight, (((1,), (1,)), ((), ())), preferred_element_type=jnp.float32
    )
    return result.reshape(values.shape[:-1] + (weight.shape[0],))


def weight_grad(left_rows, right_rows):
    return lax.dot_general(
        left_rows.reshape(-1, left_rows.shape[-1]),
        right_rows.reshape(-1, right_rows.shape[-1]),
        (((0,), (0,)), ((), ())),
        preferred_element_type=jnp.float32,
    )


def layer_norm(values, gain, shift):
    centred = values - jnp.mean(values, axis=-1, keepdims=True)
    spread = jnp.mean(centred * centred, axis=-1, keepdims=True)
    inverse = lax.rsqrt(spread + epsilon)
    scaled = centred * inverse
    return (scaled * gain + shift, scaled, inverse)


def norm_back(grad_rows, scaled, inverse, gain):
    weighted = grad_rows * gain
    result = inverse * (
        weighted
        - jnp.mean(weighted, axis=-1, keepdims=True)
        - scaled * jnp.mean(weighted * scaled, axis=-1, keepdims=True)
    )
    flat_grad = grad_rows.reshape(-1, grad_rows.shape[-1])
    flat_scaled = scaled.reshape(-1, scaled.shape[-1])
    return (result, jnp.sum(flat_grad * flat_scaled, axis=0), jnp.sum(flat_grad, axis=0))


def gelu_exact(values):
    return jax.nn.gelu(values, approximate=False)


def causal_mask(lengths_part, seq_len):
    positions = jnp.arange(seq_len)
    live_rows = positions[None, :] < lengths_part[:, None]
    return (positions[:, None] >= positions[None, :])[None] & live_rows[:, None, :]


def score_block(query_rows, key_rows, score_mask):
    score_scale = 1.0 / math.sqrt(HEAD_DIM)
    scores = (
        jnp.einsum(
            "bqhe,bkhe->bhqk",
            split_heads(query_rows),
            split_heads(key_rows),
            preferred_element_type=jnp.float32,
        )
        * score_scale
    )
    if score_mask is not None:
        scores = jnp.where(score_mask[:, None], scores, -1e30)
    return scores


def attend(query_rows, key_rows, value_rows, score_mask):
    scores = score_block(query_rows, key_rows, score_mask)
    row_peak = jnp.max(scores, axis=-1, keepdims=True)
    expanded = jnp.exp(scores - row_peak)
    row_total = jnp.sum(expanded, axis=-1, keepdims=True)
    row_probs = (expanded / row_total).astype(jnp.bfloat16)
    mixed = jnp.einsum(
        "bhqk,bkhe->bqhe", row_probs, split_heads(value_rows), preferred_element_type=jnp.float32
    )
    return (
        mixed.reshape(query_rows.shape).astype(jnp.bfloat16),
        (row_peak + jnp.log(row_total))[..., 0],
    )


def attend_back(query_rows, key_rows, value_rows, score_mask, logsum, grad_rows):
    score_scale = 1.0 / math.sqrt(HEAD_DIM)
    scores = score_block(query_rows, key_rows, score_mask)
    row_probs = jnp.exp(scores - logsum[..., None])
    grad_heads = split_heads(grad_rows)
    grad_value = jnp.einsum(
        "bhqk,bqhe->bkhe",
        row_probs.astype(jnp.bfloat16),
        grad_heads,
        preferred_element_type=jnp.float32,
    )
    grad_probs = jnp.einsum(
        "bqhe,bkhe->bhqk", grad_heads, split_heads(value_rows), preferred_element_type=jnp.float32
    )
    grad_scores = (
        row_probs * (grad_probs - jnp.sum(grad_probs * row_probs, axis=-1, keepdims=True))
    ).astype(jnp.bfloat16)
    grad_query = (
        jnp.einsum(
            "bhqk,bkhe->bqhe",
            grad_scores,
            split_heads(key_rows),
            preferred_element_type=jnp.float32,
        )
        * score_scale
    )
    grad_key = (
        jnp.einsum(
            "bhqk,bqhe->bkhe",
            grad_scores,
            split_heads(query_rows),
            preferred_element_type=jnp.float32,
        )
        * score_scale
    )
    return (
        grad_query.reshape(query_rows.shape).astype(jnp.bfloat16),
        grad_key.reshape(key_rows.shape).astype(jnp.bfloat16),
        grad_value.reshape(value_rows.shape).astype(jnp.bfloat16),
    )


def self_forward(query_rows, key_rows, value_rows, lengths_part):
    return attend(query_rows, key_rows, value_rows, causal_mask(lengths_part, query_rows.shape[1]))


def cross_forward(query_rows, key_rows, value_rows):
    return attend(query_rows, key_rows, value_rows, None)


def self_backward(query_rows, key_rows, value_rows, lengths_part, logsum, grad_rows):
    return attend_back(
        query_rows,
        key_rows,
        value_rows,
        causal_mask(lengths_part, query_rows.shape[1]),
        logsum,
        grad_rows,
    )


def cross_backward(query_rows, key_rows, value_rows, logsum, grad_rows):
    return attend_back(query_rows, key_rows, value_rows, None, logsum, grad_rows)


def blockwise(function, arrays, block_span):
    block_count = arrays[0].shape[0] // block_span

    def to_blocks(member):
        return member.reshape((block_count, block_span) + member.shape[1:])

    def from_blocks(member):
        return member.reshape((block_count * block_span,) + member.shape[2:])

    def run_block(pieces):
        return function(*pieces)

    results = lax.map(run_block, tuple((to_blocks(member) for member in arrays)))
    return jax.tree.map(from_blocks, results)


def shards(
    caption_tokens,
    image_tokens,
    caption_lengths,
    caption_image,
    norm_gain,
    norm_bias,
    self_packed,
    self_output,
    cross_query,
    cross_pair,
    cross_output,
    expand_weight,
    reduce_weight,
    cotangent,
):
    captions, seq_len, model_width = caption_tokens.shape
    peer_count = lax.axis_size("seq")
    position = lax.axis_index("seq")
    per_peer = captions // peer_count
    block_span = math.gcd(captions, max(1, 512 // seq_len))
    gathered = (
        lax.all_gather(norm_gain, ("dp", "seq"), axis=0, tiled=True),
        lax.all_gather(norm_bias, ("dp", "seq"), axis=0, tiled=True),
        lax.all_gather(self_packed, ("dp", "seq"), axis=0, tiled=True),
        lax.all_gather(self_output, ("dp", "seq"), axis=0, tiled=True),
        lax.all_gather(cross_query, ("dp", "seq"), axis=0, tiled=True),
        lax.all_gather(cross_pair, ("dp", "seq"), axis=0, tiled=True),
        lax.all_gather(cross_output, ("dp", "seq"), axis=0, tiled=True),
        lax.all_gather(expand_weight, ("dp", "seq"), axis=0, tiled=True),
        lax.all_gather(reduce_weight, ("dp", "seq"), axis=0, tiled=True),
    )
    norm_gains = gathered[0].astype(jnp.float32)
    norm_shifts = gathered[1].astype(jnp.float32)
    (
        packed_weight,
        output_weight,
        query_weight,
        pair_weight,
        cross_weight,
        expand_full,
        reduce_full,
    ) = gathered[2:]
    live_rows = jnp.arange(seq_len)[None, :] < caption_lengths[:, None]
    inputs = caption_tokens.astype(jnp.float32)
    normed_full, scaled_one, inverse_one = layer_norm(inputs, norm_gains[:, 0], norm_shifts[:, 0])
    normed_one = normed_full.astype(jnp.bfloat16)
    packed = project(normed_one, packed_weight).astype(jnp.bfloat16)
    query_part = packed[..., :model_width]
    key_part = packed[..., model_width : 2 * model_width]
    value_part = packed[..., 2 * model_width :]
    attended, logsum_one = blockwise(
        self_forward, (query_part, key_part, value_part, caption_lengths), block_span
    )
    after_self = inputs + project(attended, output_weight)
    normed_full_two, scaled_two, inverse_two = layer_norm(
        after_self, norm_gains[:, 1], norm_shifts[:, 1]
    )
    normed_two = normed_full_two.astype(jnp.bfloat16)
    routes = (caption_image // captions % peer_count).reshape(peer_count, captions)
    send_table = jnp.argsort(routes, axis=1, stable=True)
    send_order = lax.dynamic_index_in_dim(send_table, position, 0, keepdims=False)
    home_order = jnp.argsort(send_order)
    arriving = (
        lax.dynamic_slice_in_dim(send_table, position * per_peer, per_peer, 1)
        + (jnp.arange(peer_count, dtype=jnp.int32) * captions)[:, None]
    )
    image_slots = jnp.take(caption_image, arriving.reshape(-1), axis=0) % captions
    slot_order = jnp.argsort(image_slots)
    image_pair = project(image_tokens, pair_weight).astype(jnp.bfloat16)
    paired_pair = jnp.take(image_pair, image_slots, axis=0)
    paired_key = paired_pair[..., :model_width]
    paired_value = paired_pair[..., model_width:]
    outgoing = jnp.take(normed_two, send_order, axis=0)
    arrived_rows = lax.all_to_all(outgoing, "seq", split_axis=0, concat_axis=0, tiled=True)
    query_rows = project(arrived_rows, query_weight).astype(jnp.bfloat16)
    mixed_rows, logsum_rows = blockwise(
        cross_forward, (query_rows, paired_key, paired_value), block_span
    )
    branch = project(mixed_rows, cross_weight).astype(jnp.bfloat16)
    returned_rows = lax.all_to_all(branch, "seq", split_axis=0, concat_axis=0, tiled=True)
    logsum_turned = jnp.transpose(logsum_rows, (0, 2, 1))
    logsum_two = jnp.transpose(logsum_turned, (0, 2, 1))
    after_cross = after_self + jnp.take(returned_rows, home_order, axis=0).astype(jnp.float32)
    normed_full_three, scaled_three, inverse_three = layer_norm(
        after_cross, norm_gains[:, 2], norm_shifts[:, 2]
    )
    normed_three = normed_full_three.astype(jnp.bfloat16)
    gate_rows = project(normed_three, expand_full)
    hidden = gelu_exact(gate_rows).astype(jnp.bfloat16)
    caption_out = jnp.where(
        live_rows[..., None], after_cross + project(hidden, reduce_full), 0.0
    ).astype(jnp.bfloat16)
    gathered_back = (
        lax.all_gather(norm_gain, ("dp", "seq"), axis=0, tiled=True),
        lax.all_gather(norm_bias, ("dp", "seq"), axis=0, tiled=True),
        lax.all_gather(self_packed, ("dp", "seq"), axis=0, tiled=True),
        lax.all_gather(self_output, ("dp", "seq"), axis=0, tiled=True),
        lax.all_gather(cross_query, ("dp", "seq"), axis=0, tiled=True),
        lax.all_gather(cross_pair, ("dp", "seq"), axis=0, tiled=True),
        lax.all_gather(cross_output, ("dp", "seq"), axis=0, tiled=True),
        lax.all_gather(expand_weight, ("dp", "seq"), axis=0, tiled=True),
        lax.all_gather(reduce_weight, ("dp", "seq"), axis=0, tiled=True),
    )
    gains_back = gathered_back[0].astype(jnp.float32)
    packed_back, output_back, query_back, pair_back, cross_back, expand_back, reduce_back = (
        gathered_back[2:]
    )
    grad_out = jnp.where(live_rows[..., None], cotangent, jnp.zeros_like(cotangent))
    reduce_grad = weight_grad(hidden, grad_out)
    _, gelu_pull = jax.vjp(gelu_exact, gate_rows)
    grad_gate = gelu_pull(project_back(grad_out, reduce_back))[0].astype(jnp.bfloat16)
    expand_grad = weight_grad(normed_three, grad_gate)
    grad_norm_three, gain_three, shift_three = norm_back(
        project_back(grad_gate, expand_back), scaled_three, inverse_three, gains_back[:, 2]
    )
    grad_second = grad_out.astype(jnp.float32) + grad_norm_three
    grad_branch = grad_second.astype(jnp.bfloat16)
    grad_arrived = lax.all_to_all(
        jnp.take(grad_branch, send_order, axis=0), "seq", split_axis=0, concat_axis=0, tiled=True
    )
    cross_output_grad = weight_grad(mixed_rows, grad_arrived)
    grad_cross_mixed = project_back(grad_arrived, cross_back).astype(jnp.bfloat16)
    grad_cross_rows, grad_image_key, grad_image_value = blockwise(
        cross_backward,
        (query_rows, paired_key, paired_value, logsum_two, grad_cross_mixed),
        block_span,
    )
    grad_pair = jnp.take(
        jnp.concatenate([grad_image_key, grad_image_value], axis=-1), slot_order, axis=0
    )
    cross_pair_grad = weight_grad(image_tokens, grad_pair)
    image_grad = project_back(grad_pair, pair_back).astype(jnp.bfloat16)
    cross_query_grad = weight_grad(arrived_rows, grad_cross_rows)
    grad_home = lax.all_to_all(
        project_back(grad_cross_rows, query_back).astype(jnp.bfloat16),
        "seq",
        split_axis=0,
        concat_axis=0,
        tiled=True,
    )
    grad_norm_two, gain_two, shift_two = norm_back(
        jnp.take(grad_home, home_order, axis=0).astype(jnp.float32),
        scaled_two,
        inverse_two,
        gains_back[:, 1],
    )
    grad_first = grad_second + grad_norm_two
    grad_self = grad_first.astype(jnp.bfloat16)
    self_output_grad = weight_grad(attended, grad_self)
    grad_attended = project_back(grad_self, output_back).astype(jnp.bfloat16)
    grad_query, grad_key, grad_value = blockwise(
        self_backward,
        (query_part, key_part, value_part, caption_lengths, logsum_one, grad_attended),
        block_span,
    )
    grad_packed = jnp.concatenate([grad_query, grad_key, grad_value], axis=-1)
    self_packed_grad = weight_grad(normed_one, grad_packed)
    grad_norm_one, gain_one, shift_one = norm_back(
        project_back(grad_packed, packed_back), scaled_one, inverse_one, gains_back[:, 0]
    )
    caption_grad = (grad_first + grad_norm_one).astype(jnp.bfloat16)
    gain_stack = jnp.stack([gain_one, gain_two, gain_three], axis=1)
    shift_stack = jnp.stack([shift_one, shift_two, shift_three], axis=1)
    group_sums = (
        lax.psum_scatter(gain_stack, "dp", scatter_dimension=0, tiled=True),
        lax.psum_scatter(shift_stack, "dp", scatter_dimension=0, tiled=True),
        lax.psum_scatter(self_packed_grad, "dp", scatter_dimension=0, tiled=True),
        lax.psum_scatter(self_output_grad, "dp", scatter_dimension=0, tiled=True),
        lax.psum_scatter(cross_query_grad, "dp", scatter_dimension=0, tiled=True),
        lax.psum_scatter(cross_pair_grad, "dp", scatter_dimension=0, tiled=True),
        lax.psum_scatter(cross_output_grad, "dp", scatter_dimension=0, tiled=True),
        lax.psum_scatter(expand_grad, "dp", scatter_dimension=0, tiled=True),
        lax.psum_scatter(reduce_grad, "dp", scatter_dimension=0, tiled=True),
    )
    summed = (
        lax.psum_scatter(
            group_sums[0].astype(jnp.bfloat16), "seq", scatter_dimension=0, tiled=True
        ).astype(jnp.float32),
        lax.psum_scatter(
            group_sums[1].astype(jnp.bfloat16), "seq", scatter_dimension=0, tiled=True
        ).astype(jnp.float32),
        lax.psum_scatter(
            group_sums[2].astype(jnp.bfloat16), "seq", scatter_dimension=0, tiled=True
        ).astype(jnp.float32),
        lax.psum_scatter(
            group_sums[3].astype(jnp.bfloat16), "seq", scatter_dimension=0, tiled=True
        ).astype(jnp.float32),
        lax.psum_scatter(
            group_sums[4].astype(jnp.bfloat16), "seq", scatter_dimension=0, tiled=True
        ).astype(jnp.float32),
        lax.psum_scatter(
            group_sums[5].astype(jnp.bfloat16), "seq", scatter_dimension=0, tiled=True
        ).astype(jnp.float32),
        lax.psum_scatter(
            group_sums[6].astype(jnp.bfloat16), "seq", scatter_dimension=0, tiled=True
        ).astype(jnp.float32),
        lax.psum_scatter(
            group_sums[7].astype(jnp.bfloat16), "seq", scatter_dimension=0, tiled=True
        ).astype(jnp.float32),
        lax.psum_scatter(
            group_sums[8].astype(jnp.bfloat16), "seq", scatter_dimension=0, tiled=True
        ).astype(jnp.float32),
    )
    return (
        caption_out,
        caption_grad,
        image_grad,
        summed[0],
        summed[1],
        summed[2],
        summed[3],
        summed[4],
        summed[5],
        summed[6],
        summed[7],
        summed[8],
    )


def solution(mesh):
    placed = (
        P(("dp", "seq"), None, None),
        P(("dp", "seq"), None, None),
        P(("dp", "seq")),
        P("dp"),
        P(("dp", "seq"), None),
        P(("dp", "seq"), None),
        P(("dp", "seq"), None),
        P(("dp", "seq"), None),
        P(("dp", "seq"), None),
        P(("dp", "seq"), None),
        P(("dp", "seq"), None),
        P(("dp", "seq"), None),
        P(("dp", "seq"), None),
        P(("dp", "seq"), None, None),
    )
    return jax.shard_map(
        shards,
        mesh=mesh,
        in_specs=placed,
        out_specs=(
            P(("dp", "seq"), None, None),
            P(("dp", "seq"), None, None),
            P(("dp", "seq"), None, None),
            P(("dp", "seq"), None),
            P(("dp", "seq"), None),
            P(("dp", "seq"), None),
            P(("dp", "seq"), None),
            P(("dp", "seq"), None),
            P(("dp", "seq"), None),
            P(("dp", "seq"), None),
            P(("dp", "seq"), None),
            P(("dp", "seq"), None),
        ),
        check_vma=False,
    )
```

profile of v0, /device:TPU:0, one launch (start us, length us, event | category | flops | bytes accessed | tf_op | source)
XLA Modules:
  0.0 1545.0 jit_solution(144113735227643200)
XLA Ops:
  18.0 43.5 %all-gather = bf16[32,24,3]{1,2,0:T(4,128)(2,1)S(1)} all-gather(bf16[1,24,3]{1,2,0:T(4,128)(2,1)S(1)} %bitcast.230), channel_id=1, replica_groups=mesh['dp'=8,'seq'=4] {'dp','seq'}, dimensions={0}, use_global_device_ids=true | all-gather | bytes 4752 | tf_op jit(solution)/shard_map/all_gather | solution.py:207
  61.8 36.7 %all-gather.1 = bf16[32,24,3]{1,2,0:T(4,128)(2,1)S(1)} all-gather(bf16[1,24,3]{1,2,0:T(4,128)(2,1)S(1)} %bitcast.231), channel_id=1, replica_groups=mesh['dp'=8,'seq'=4] {'dp','seq'}, dimensions={0}, use_global_device_ids=true | all-gather | bytes 4752 | tf_op jit(solution)/shard_map/all_gather | solution.py:208
  108.1 24.4 %all-gather.10.cloned.1.call-done = bf16[768,2304]{1,0:T(8,128)(2,1)} async-done(((bf16[24,2304]{1,0:T(8,128)(2,1)}), bf16[768,2304]{1,0:T(8,128)(2,1)}) %all-gather.10.cloned.1.call-update) | async-done | bytes 3538960 | tf_op jit(solution)/shard_map/all_gather | solution.py:209
  144.2 43.9 %all-gather.12.cloned.1.call-done = bf16[768,768]{1,0:T(8,128)(2,1)} async-done(((bf16[24,768]{1,0:T(8,128)(2,1)}), bf16[768,768]{1,0:T(8,128)(2,1)}) %all-gather.12.cloned.1.call-update) | async-done | bytes 1179664 | tf_op jit(solution)/shard_map/all_gather | solution.py:210
  205.3 38.6 %all-gather.16.cloned.1.call-done = bf16[768,768]{1,0:T(8,128)(2,1)} async-done(((bf16[24,768]{1,0:T(8,128)(2,1)}), bf16[768,768]{1,0:T(8,128)(2,1)}) %all-gather.16.cloned.1.call-update) | async-done | bytes 1179664 | tf_op jit(solution)/shard_map/all_gather | solution.py:211
  256.0 43.6 %all-gather.18.cloned.1.call-done = bf16[768,768]{1,0:T(8,128)(2,1)} async-done(((bf16[24,768]{1,0:T(8,128)(2,1)}), bf16[768,768]{1,0:T(8,128)(2,1)}) %all-gather.18.cloned.1.call-update) | async-done | bytes 1179664 | tf_op jit(solution)/shard_map/all_gather | solution.py:213
  306.9 11.8 all-to-all-done.1
  321.6 43.9 %all-gather.20.cloned.1.call-done = bf16[768,3072]{1,0:T(8,128)(2,1)} async-done(((bf16[24,3072]{1,0:T(8,128)(2,1)}), bf16[768,3072]{1,0:T(8,128)(2,1)}) %all-gather.20.cloned.1.call-update) | async-done | bytes 4718608 | tf_op jit(solution)/shard_map/all_gather | solution.py:214
  374.5 15.1 multiply_convert_fusion
  389.6 40.8 %all-gather.22.cloned.1.call-done = bf16[3072,768]{1,0:T(8,128)(2,1)} async-done(((bf16[96,768]{1,0:T(8,128)(2,1)}), bf16[3072,768]{1,0:T(8,128)(2,1)}) %all-gather.22.cloned.1.call-update) | async-done | bytes 4718608 | tf_op jit(solution)/shard_map/all_gather | solution.py:215
  430.4 10.2 add_convert_fusion
  454.1 14.4 all_to_all.20
  492.7 14.8 all_to_all.21
  541.2 6.9 convolution_bitcast_fusion.3
  582.1 7.0 convolution_bitcast_fusion
  589.2 7.0 convolution_bitcast_fusion.2
  597.5 8.2 convolution_bitcast_fusion.1
  620.1 64.3 %reduce-scatter.31.cloned.1.call-done = f32[96,768]{1,0:T(8,128)} async-done(((f32[768,768]{1,0:T(8,128)}), f32[96,768]{1,0:T(8,128)}) %reduce-scatter.31.cloned.1.call-update) | async-done | bytes 294928 | tf_op jit(solution)/shard_map/reduce_scatter | solution.py:353
  686.1 96.9 %reduce-scatter.55.cloned.1.call-done = f32[96,1536]{1,0:T(8,128)} async-done(((f32[768,1536]{1,0:T(8,128)}), f32[96,1536]{1,0:T(8,128)}) %reduce-scatter.55.cloned.1.call-update) | async-done | bytes 589840
  785.2 130.1 %reduce-scatter.27.cloned.1.call-done = f32[96,2304]{1,0:T(8,128)} async-done(((f32[768,2304]{1,0:T(8,128)}), f32[96,2304]{1,0:T(8,128)}) %reduce-scatter.27.cloned.1.call-update) | async-done | bytes 884752 | tf_op jit(solution)/shard_map/reduce_scatter | solution.py:352
  917.3 162.8 %reduce-scatter.43.cloned.1.call-done = f32[96,3072]{1,0:T(8,128)} async-done(((f32[768,3072]{1,0:T(8,128)}), f32[96,3072]{1,0:T(8,128)}) %reduce-scatter.43.cloned.1.call-update) | async-done | bytes 1179664 | tf_op jit(solution)/shard_map/reduce_scatter | solution.py:357
  1083.7 6.8 select_convert_fusion
  1090.5 154.4 %reduce-scatter.47.cloned.1.call-done = f32[384,768]{1,0:T(8,128)} async-done(((f32[3072,768]{1,0:T(8,128)}), f32[384,768]{1,0:T(8,128)}) %reduce-scatter.47.cloned.1.call-update) | async-done | bytes 1179664 | tf_op jit(solution)/shard_map/reduce_scatter | solution.py:358
  1254.7 54.5 %reduce-scatter.51.cloned.1.call-done = f32[96,3]{1,0:T(8,128)} async-done(((f32[768,3]{1,0:T(8,128)}), f32[96,3]{1,0:T(8,128)}) %reduce-scatter.51.cloned.1.call-update) | async-done | bytes 1168
  1310.1 63.5 %reduce-scatter.53.cloned.1.call-done = f32[96,3]{1,0:T(8,128)} async-done(((f32[768,3]{1,0:T(8,128)}), f32[96,3]{1,0:T(8,128)}) %reduce-scatter.53.cloned.1.call-update) | async-done | bytes 1168
  1381.5 13.8 reduce-scatter.41.cloned.1.call-done
  1396.6 21.2 %reduce-scatter.37.cloned.1.call-done = bf16[24,768]{1,0:T(8,128)(2,1)} async-done(((bf16[96,768]{1,0:T(8,128)(2,1)}), bf16[24,768]{1,0:T(8,128)(2,1)}) %reduce-scatter.37.cloned.1.call-update) | async-done | bytes 36880 | tf_op jit(solution)/shard_map/reduce_scatter | solution.py:373
  1419.2 21.3 %reduce-scatter.33.cloned.1.call-done = bf16[24,768]{1,0:T(8,128)(2,1)} async-done(((bf16[96,768]{1,0:T(8,128)(2,1)}), bf16[24,768]{1,0:T(8,128)(2,1)}) %reduce-scatter.33.cloned.1.call-update) | async-done | bytes 36880 | tf_op jit(solution)/shard_map/reduce_scatter | solution.py:370
  1441.9 21.8 %reduce-scatter.57.cloned.1.call-done = bf16[24,1536]{1,0:T(8,128)(2,1)} async-done(((bf16[96,1536]{1,0:T(8,128)(2,1)}), bf16[24,1536]{1,0:T(8,128)(2,1)}) %reduce-scatter.57.cloned.1.call-update) | async-done | bytes 73744
  1465.7 21.7 %reduce-scatter.29.cloned.1.call-done = bf16[24,2304]{1,0:T(8,128)(2,1)} async-done(((bf16[96,2304]{1,0:T(8,128)(2,1)}), bf16[24,2304]{1,0:T(8,128)(2,1)}) %reduce-scatter.29.cloned.1.call-update) | async-done | bytes 110608 | tf_op jit(solution)/shard_map/reduce_scatter | solution.py:367
  1489.0 23.0 %reduce-scatter.45.cloned.1.call-done = bf16[24,3072]{1,0:T(8,128)(2,1)} async-done(((bf16[96,3072]{1,0:T(8,128)(2,1)}), bf16[24,3072]{1,0:T(8,128)(2,1)}) %reduce-scatter.45.cloned.1.call-update) | async-done | bytes 147472 | tf_op jit(solution)/shard_map/reduce_scatter | solution.py:382
  1513.6 22.9 %reduce-scatter.49.cloned.1.call-done = bf16[96,768]{1,0:T(8,128)(2,1)} async-done(((bf16[384,768]{1,0:T(8,128)(2,1)}), bf16[96,768]{1,0:T(8,128)(2,1)}) %reduce-scatter.49.cloned.1.call-update) | async-done | bytes 147472 | tf_op jit(solution)/shard_map/reduce_scatter | solution.py:385
  (312 shorter events, 239.1 us)
Async XLA Ops:
  7.2 54.5 %copy-start.42 = (bf16[24,3]{0,1:T(4,128)(2,1)S(1)}, bf16[24,3]{0,1:T(4,128)(2,1)}, u32[]{:S(2)}) copy-start(bf16[24,3]{0,1:T(4,128)(2,1)} %param.23) | copy-start | bytes 436
  7.2 91.8 %copy-start.44 = (bf16[4,196,768]{2,0,1:T(4,128)(2,1)S(1)}, bf16[4,196,768]{2,0,1:T(4,128)(2,1)}, u32[]{:S(2)}) copy-start(bf16[4,196,768]{2,0,1:T(4,128)(2,1)} %param.19) | copy-start | bytes 3612676
  7.2 91.8 %all-gather.14.cloned.1.call-start = ((), (), s32[]{:S(2)}) async-start(), calls=%async_computation.22 | async-start | bytes 2433024 | tf_op jit(solution)/shard_map/all_gather | solution.py:212
  8.0 124.5 %all-gather.10.cloned.1.call-start = ((), (), s32[]{:S(2)}) async-start(), calls=%async_computation.20 | async-start | bytes 3649536 | tf_op jit(solution)/shard_map/all_gather | solution.py:209
  8.7 179.5 %all-gather.12.cloned.1.call-start = ((), (), s32[]{:S(2)}) async-start(), calls=%async_computation.21 | async-start | bytes 1216512 | tf_op jit(solution)/shard_map/all_gather | solution.py:210
  9.4 234.4 %all-gather.16.cloned.1.call-start = ((), (), s32[]{:S(2)}) async-start(), calls=%async_computation.23 | async-start | bytes 1216512 | tf_op jit(solution)/shard_map/all_gather | solution.py:211
  10.0 289.5 %all-gather.18.cloned.1.call-start = ((), (), s32[]{:S(2)}) async-start(), calls=%async_computation.24 | async-start | bytes 1216512 | tf_op jit(solution)/shard_map/all_gather | solution.py:213
  10.6 355.0 %all-gather.20.cloned.1.call-start = ((), (), s32[]{:S(2)}) async-start(), calls=%async_computation.25 | async-start | bytes 4866048 | tf_op jit(solution)/shard_map/all_gather | solution.py:214
  11.2 419.2 %all-gather.22.cloned.1.call-start = ((), (), s32[]{:S(2)}) async-start(), calls=%async_computation.26 | async-start | bytes 4866048 | tf_op jit(solution)/shard_map/all_gather | solution.py:215
  14.4 581.9 %copy-start.39 = (pred[4,128]{1,0:T(4,128)(4,1)}, pred[4,128]{1,0:T(4,128)(4,1)S(1)}, u32[]{:S(2)}) copy-start(pred[4,128]{1,0:T(4,128)(4,1)S(1)} %iota_compare_fusion.1) | copy-start | bytes 1540
  192.6 51.3 %all-to-all-start = ((bf16[4,128,768]{2,1,0:T(8,128)(2,1)}), bf16[4,128,768]{2,1,0:T(8,128)(2,1)}, u32[]{:S(2)}, u32[]{:S(2)}) async-start(bf16[4,128,768]{2,1,0:T(8,128)(2,1)} %broadcast_select_fusion.6), calls=%async_computation | async-start | bytes 1572864 | tf_op jit(solution)/shard_map/all_to_all | solution.py:259
  302.5 16.1 %all-to-all-start.1 = ((bf16[4,128,768]{2,1,0:T(8,128)(2,1)}), bf16[4,128,768]{2,1,0:T(8,128)(2,1)S(1)}, u32[]{:S(2)}, u32[]{:S(2)}) async-start(bf16[4,128,768]{2,1,0:T(8,128)(2,1)} %convolution_convert_fusion.5), calls=%async_computation.1 | async-start | bytes 1572864 | tf_op jit(solution)/shard_map/all_to_all | solution.py:265
  306.0 310.6 %reduce-scatter.39.cloned.1.call-start = ((), (), s32[]{:S(2)}) async-start(), calls=%async_computation.33 | async-start | bytes 2654208 | tf_op jit(solution)/shard_map/reduce_scatter | solution.py:356
  471.7 146.6 %reduce-scatter.35.cloned.1.call-start = ((), (), s32[]{:S(2)}) async-start(), calls=%async_computation.31 | async-start | bytes 2654208 | tf_op jit(solution)/shard_map/reduce_scatter | solution.py:354
  490.2 194.1 %reduce-scatter.31.cloned.1.call-start = ((), (), s32[]{:S(2)}) async-start(), calls=%async_computation.29 | async-start | bytes 2654208 | tf_op jit(solution)/shard_map/reduce_scatter | solution.py:353
  517.8 265.1 %reduce-scatter.55.cloned.1.call-start = ((), (), s32[]{:S(2)}) async-start(), calls=%async_computation.41 | async-start | bytes 5308416
  554.2 361.1 %reduce-scatter.27.cloned.1.call-start = ((), (), s32[]{:S(2)}) async-start(), calls=%async_computation.27 | async-start | bytes 7962624 | tf_op jit(solution)/shard_map/reduce_scatter | solution.py:352
  589.1 491.0 %reduce-scatter.43.cloned.1.call-start = ((), (), s32[]{:S(2)}) async-start(), calls=%async_computation.35 | async-start | bytes 10616832 | tf_op jit(solution)/shard_map/reduce_scatter | solution.py:357
  596.2 648.6 %reduce-scatter.47.cloned.1.call-start = ((), (), s32[]{:S(2)}) async-start(), calls=%async_computation.37 | async-start | bytes 10616832 | tf_op jit(solution)/shard_map/reduce_scatter | solution.py:358
  605.8 703.5 %reduce-scatter.51.cloned.1.call-start = ((), (), s32[]{:S(2)}) async-start(), calls=%async_computation.39 | async-start | bytes 442368
  615.5 758.1 %reduce-scatter.53.cloned.1.call-start = ((), (), s32[]{:S(2)}) async-start(), calls=%async_computation.40 | async-start | bytes 442368
  616.5 778.7 %reduce-scatter.41.cloned.1.call-start = ((), (), s32[]{:S(2)}) async-start(), calls=%async_computation.34 | async-start | bytes 184320 | tf_op jit(solution)/shard_map/reduce_scatter | solution.py:379
  618.3 799.5 %reduce-scatter.37.cloned.1.call-start = ((), (), s32[]{:S(2)}) async-start(), calls=%async_computation.32 | async-start | bytes 184320 | tf_op jit(solution)/shard_map/reduce_scatter | solution.py:373
  620.0 820.5 %reduce-scatter.33.cloned.1.call-start = ((), (), s32[]{:S(2)}) async-start(), calls=%async_computation.30 | async-start | bytes 184320 | tf_op jit(solution)/shard_map/reduce_scatter | solution.py:370
  686.0 777.7 %reduce-scatter.57.cloned.1.call-start = ((), (), s32[]{:S(2)}) async-start(), calls=%async_computation.42 | async-start | bytes 368640
  784.2 299.5 %copy-start.17 = (bf16[4,128,768]{2,1,0:T(8,128)(2,1)S(1)}, bf16[4,128,768]{2,1,0:T(8,128)(2,1)}, u32[]{:S(2)}) copy-start(bf16[4,128,768]{2,1,0:T(8,128)(2,1)} %copy-done.16) | copy-start | bytes 2359300
  785.1 297.3 %copy-start.45 = (u32[32]{0:T(128)S(1)}, u32[32]{0:T(128)}, u32[]{:S(2)}) copy-start(u32[32]{0:T(128)} %constant.260) | copy-start | bytes 388
  785.1 298.6 %copy-start.40 = (pred[4,128]{1,0:T(4,128)(4,1)S(1)}, pred[4,128]{1,0:T(4,128)(4,1)}, u32[]{:S(2)}) copy-start(pred[4,128]{1,0:T(4,128)(4,1)} %copy-done.39) | copy-start | bytes 1540
  785.1 702.3 %reduce-scatter.29.cloned.1.call-start = ((), (), s32[]{:S(2)}) async-start(), calls=%async_computation.28 | async-start | bytes 552960 | tf_op jit(solution)/shard_map/reduce_scatter | solution.py:367
  917.3 594.7 %reduce-scatter.45.cloned.1.call-start = ((), (), s32[]{:S(2)}) async-start(), calls=%async_computation.36 | async-start | bytes 737280 | tf_op jit(solution)/shard_map/reduce_scatter | solution.py:382
  1082.4 454.2 %reduce-scatter.49.cloned.1.call-start = ((), (), s32[]{:S(2)}) async-start(), calls=%async_computation.38 | async-start | bytes 737280 | tf_op jit(solution)/shard_map/reduce_scatter | solution.py:385
  1083.7 163.3 %copy-start.47 = (pred[4]{0:T(512)(128)(4,1)S(1)}, pred[4]{0:T(512)(128)(4,1)}, u32[]{:S(2)}) copy-start(pred[4]{0:T(512)(128)(4,1)} %copy-done.46) | copy-start | bytes 16
  (43 other events, 322.3 us)
Sparse Core Ops, SparseCore 0:
  10.9 59.7 all-gather.13
  73.6 58.8 all-gather.9
  135.4 52.7 all-gather.11
  190.9 52.9 all-gather.15
  246.6 52.8 all-gather.17
  302.3 63.1 all-gather.19
  368.5 61.9 all-gather.21
  471.8 67.8 reduce-scatter.38
  543.2 68.8 reduce-scatter.34
  615.5 68.7 reduce-scatter.30
  688.0 94.8 reduce-scatter.54
  786.5 128.7 reduce-scatter.26
  918.9 161.2 reduce-scatter.42
  1083.6 161.1 reduce-scatter.46
  1248.0 61.2 reduce-scatter.50
  1312.4 61.2 reduce-scatter.52
  1376.5 18.6 reduce-scatter.40
  1398.1 19.6 reduce-scatter.36
  1420.8 19.6 reduce-scatter.32
  1443.4 20.2 reduce-scatter.56
  1466.3 21.0 reduce-scatter.28
  1489.9 22.0 reduce-scatter.44
  1514.5 22.0 reduce-scatter.48
where the time goes:
time: 1560 us; the launch traced here: 1540 us
  waiting for transfers between devices  1120 us (72%)
  matrix products  134 us (9%)
  blocking collectives  115 us (7%)
  local copies, waits for them, and re-layouts  78.9 us (5%)
  other arithmetic  67.7 us (4%)
  between operations  15.9 us (1%)
    unnamed x27, waiting for transfers between devices  241 us
    reduce_scatter x1, waiting for transfers between devices, shards(): lax.psum_scatter(expand_grad, 'dp', scatter_dimension=0, tiled=True)  163 us
    reduce_scatter x1, waiting for transfers between devices, shards(): lax.psum_scatter(reduce_grad, 'dp', scatter_dimension=0, tiled=True)  154 us
    reduce_scatter x1, waiting for transfers between devices, shards(): lax.psum_scatter(self_packed_grad, 'dp', scatter_dimension=0, tiled=True)  130 us
    reduce_scatter x1, waiting for transfers between devices, shards(): lax.psum_scatter(self_output_grad, 'dp', scatter_dimension=0, tiled=True)  64.3 us
    all_gather x1, waiting for transfers between devices, shards(): lax.all_gather(self_output, ('dp', 'seq'), axis=0, tiled=True)  43.9 us
    all_gather x1, waiting for transfers between devices, shards(): lax.all_gather(expand_weight, ('dp', 'seq'), axis=0, tiled=True)  43.9 us
    all_gather x1, waiting for transfers between devices, shards(): lax.all_gather(cross_output, ('dp', 'seq'), axis=0, tiled=True)  43.6 us
  transfers between devices with their start and end apart: 25, of which 21 were waited for; matrix products, arithmetic and copies ran while one was open for 15% of the time, Pallas kernels for 0%

commit v1 on v0

v1 whole, which is shorter than its diff:
```python
import math

import jax
import jax.numpy as jnp
from jax import lax
from jax.sharding import PartitionSpec as P

HEADS = 12
HEAD_DIM = 64


epsilon = 1e-05


def split_heads(values):
    return values.reshape(values.shape[:-1] + (HEADS, HEAD_DIM))


def project(values, weight):
    flat_rows = values.reshape(-1, values.shape[-1])
    return jnp.dot(flat_rows, weight, preferred_element_type=jnp.float32).reshape(
        values.shape[:-1] + (weight.shape[1],)
    )


def project_back(values, weight):
    flat_rows = values.reshape(-1, values.shape[-1])
    result = lax.dot_general(
        flat_rows, weight, (((1,), (1,)), ((), ())), preferred_element_type=jnp.float32
    )
    return result.reshape(values.shape[:-1] + (weight.shape[0],))


def weight_grad(left_rows, right_rows):
    return lax.dot_general(
        left_rows.reshape(-1, left_rows.shape[-1]),
        right_rows.reshape(-1, right_rows.shape[-1]),
        (((0,), (0,)), ((), ())),
        preferred_element_type=jnp.float32,
    )


def layer_norm(values, gain, shift):
    centred = values - jnp.mean(values, axis=-1, keepdims=True)
    spread = jnp.mean(centred * centred, axis=-1, keepdims=True)
    inverse = lax.rsqrt(spread + epsilon)
    scaled = centred * inverse
    return (scaled * gain + shift, scaled, inverse)


def norm_back(grad_rows, scaled, inverse, gain):
    weighted = grad_rows * gain
    result = inverse * (
        weighted
        - jnp.mean(weighted, axis=-1, keepdims=True)
        - scaled * jnp.mean(weighted * scaled, axis=-1, keepdims=True)
    )
    flat_grad = grad_rows.reshape(-1, grad_rows.shape[-1])
    flat_scaled = scaled.reshape(-1, scaled.shape[-1])
    return (result, jnp.sum(flat_grad * flat_scaled, axis=0), jnp.sum(flat_grad, axis=0))


def gelu_exact(values):
    return jax.nn.gelu(values, approximate=False)


def causal_mask(lengths_part, seq_len):
    positions = jnp.arange(seq_len)
    live_rows = positions[None, :] < lengths_part[:, None]
    return (positions[:, None] >= positions[None, :])[None] & live_rows[:, None, :]


def score_block(query_rows, key_rows, score_mask):
    score_scale = 1.0 / math.sqrt(HEAD_DIM)
    scores = (
        jnp.einsum(
            "bqhe,bkhe->bhqk",
            split_heads(query_rows),
            split_heads(key_rows),
            preferred_element_type=jnp.float32,
        )
        * score_scale
    )
    if score_mask is not None:
        scores = jnp.where(score_mask[:, None], scores, -1e30)
    return scores


def attend(query_rows, key_rows, value_rows, score_mask):
    scores = score_block(query_rows, key_rows, score_mask)
    row_peak = jnp.max(scores, axis=-1, keepdims=True)
    expanded = jnp.exp(scores - row_peak)
    row_total = jnp.sum(expanded, axis=-1, keepdims=True)
    row_probs = (expanded / row_total).astype(jnp.bfloat16)
    mixed = jnp.einsum(
        "bhqk,bkhe->bqhe", row_probs, split_heads(value_rows), preferred_element_type=jnp.float32
    )
    return (
        mixed.reshape(query_rows.shape).astype(jnp.bfloat16),
        (row_peak + jnp.log(row_total))[..., 0],
    )


def attend_back(query_rows, key_rows, value_rows, score_mask, logsum, grad_rows):
    score_scale = 1.0 / math.sqrt(HEAD_DIM)
    scores = score_block(query_rows, key_rows, score_mask)
    row_probs = jnp.exp(scores - logsum[..., None])
    grad_heads = split_heads(grad_rows)
    grad_value = jnp.einsum(
        "bhqk,bqhe->bkhe",
        row_probs.astype(jnp.bfloat16),
        grad_heads,
        preferred_element_type=jnp.float32,
    )
    grad_probs = jnp.einsum(
        "bqhe,bkhe->bhqk", grad_heads, split_heads(value_rows), preferred_element_type=jnp.float32
    )
    grad_scores = (
        row_probs * (grad_probs - jnp.sum(grad_probs * row_probs, axis=-1, keepdims=True))
    ).astype(jnp.bfloat16)
    grad_query = (
        jnp.einsum(
            "bhqk,bkhe->bqhe",
            grad_scores,
            split_heads(key_rows),
            preferred_element_type=jnp.float32,
        )
        * score_scale
    )
    grad_key = (
        jnp.einsum(
            "bhqk,bqhe->bkhe",
            grad_scores,
            split_heads(query_rows),
            preferred_element_type=jnp.float32,
        )
        * score_scale
    )
    return (
        grad_query.reshape(query_rows.shape).astype(jnp.bfloat16),
        grad_key.reshape(key_rows.shape).astype(jnp.bfloat16),
        grad_value.reshape(value_rows.shape).astype(jnp.bfloat16),
    )


def self_forward(query_rows, key_rows, value_rows, lengths_part):
    return attend(query_rows, key_rows, value_rows, causal_mask(lengths_part, query_rows.shape[1]))


def cross_forward(query_rows, key_rows, value_rows):
    return attend(query_rows, key_rows, value_rows, None)


def self_backward(query_rows, key_rows, value_rows, lengths_part, logsum, grad_rows):
    return attend_back(
        query_rows,
        key_rows,
        value_rows,
        causal_mask(lengths_part, query_rows.shape[1]),
        logsum,
        grad_rows,
    )


def cross_backward(query_rows, key_rows, value_rows, logsum, grad_rows):
    return attend_back(query_rows, key_rows, value_rows, None, logsum, grad_rows)


def index_bits():
    found = []
    for axis in ("dp", "seq"):
        count = lax.axis_size(axis)
        found += [(axis, bit) for bit in reversed(range(count.bit_length() - 1))]
    return found


def swap_pairs(axis, bit):
    return [(i, i ^ (1 << bit)) for i in range(lax.axis_size(axis))]


def own_bit(axis, bit):
    return (lax.axis_index(axis) >> bit) & 1


def gather_order(flip):
    far = [("dp", bit) for bit in range(1, lax.axis_size("dp").bit_length() - 1)]
    near = [[("dp", 0)], [("seq", bit) for bit in range(1, lax.axis_size("seq").bit_length() - 1)]]
    if flip:
        near = near[::-1]
    return far + near[0] + near[1] + [("seq", 0)]


def gather_rows(part, flip):
    bits = index_bits()
    state = part.reshape((1,) * len(bits) + part.shape)
    for place in gather_order(flip):
        dim = bits.index(place)
        other = lax.ppermute(state, place[0], swap_pairs(*place))
        state = jnp.where(
            own_bit(*place) == 0,
            jnp.concatenate([state, other], dim),
            jnp.concatenate([other, state], dim),
        )
    return state.reshape((-1,) + part.shape[1:])


def scatter_rows(whole, flip):
    bits = index_bits()
    rows = whole.shape[0] >> len(bits)
    state = whole.reshape((2,) * len(bits) + (rows,) + whole.shape[1:])
    order = gather_order(flip)
    for place in [order[-1]] + order[:-1][::-1]:
        dim = bits.index(place)
        mine = own_bit(*place)
        given = lax.dynamic_slice_in_dim(state, 1 - mine, 1, dim)
        kept = lax.dynamic_slice_in_dim(state, mine, 1, dim)
        state = kept + lax.ppermute(given, place[0], swap_pairs(*place))
    return state.reshape((rows,) + whole.shape[1:])


def route(table_rows, pick, place):
    peers = lax.axis_size("seq")
    position = lax.axis_index("seq")
    arrived = []
    for k in range(peers):
        rows = jnp.take(table_rows, pick[position ^ k], axis=0)
        if k:
            rows = lax.ppermute(rows, "seq", [(i, i ^ k) for i in range(peers)])
        arrived.append(rows)
    return jnp.take(jnp.concatenate(arrived, axis=0), place, axis=0)


def shards(
    caption_tokens,
    image_tokens,
    caption_lengths,
    caption_image,
    norm_gain,
    norm_bias,
    self_packed,
    self_output,
    cross_query,
    cross_pair,
    cross_output,
    expand_weight,
    reduce_weight,
    cotangent,
):
    captions, seq_len, model_width = caption_tokens.shape
    peer_count = lax.axis_size("seq")
    position = lax.axis_index("seq")
    per_peer = captions // peer_count

    owner = (caption_image // captions % peer_count).reshape(peer_count, captions)
    slot = (caption_image % captions).reshape(peer_count, captions)
    by_owner = jnp.argsort(owner, axis=1, stable=True).reshape(peer_count, peer_count, per_peer)
    slot_by_owner = jnp.take_along_axis(
        slot, by_owner.reshape(peer_count, captions), axis=1
    ).reshape(peer_count, peer_count, per_peer)
    asked = slot_by_owner[:, position]
    held = by_owner[position]
    turns = position ^ jnp.arange(peer_count)
    image_place = jnp.argsort(held[turns].reshape(-1))
    home_place = jnp.argsort(asked[turns].reshape(-1))
    paired = route(image_tokens, asked, image_place)

    norm_columns = jnp.pad(jnp.concatenate([norm_gain, norm_bias], axis=1), ((0, 0), (0, 122)))
    first_group = gather_rows(jnp.concatenate([self_packed, norm_columns], axis=1), False)
    second_group = gather_rows(
        jnp.concatenate([cross_pair, self_output, cross_query, cross_output], axis=1), True
    )
    expand_full = gather_rows(expand_weight, False)
    reduce_full = gather_rows(reduce_weight, True)
    packed_weight = first_group[:, : 3 * model_width]
    norm_values = first_group[:, 3 * model_width : 3 * model_width + 6].astype(jnp.float32)
    norm_gains, norm_shifts = norm_values[:, :3], norm_values[:, 3:]
    pair_weight = second_group[:, : 2 * model_width]
    output_weight = second_group[:, 2 * model_width : 3 * model_width]
    query_weight = second_group[:, 3 * model_width : 4 * model_width]
    cross_weight = second_group[:, 4 * model_width :]

    live_rows = jnp.arange(seq_len)[None, :] < caption_lengths[:, None]
    inputs = caption_tokens.astype(jnp.float32)
    normed_full, scaled_one, inverse_one = layer_norm(inputs, norm_gains[:, 0], norm_shifts[:, 0])
    normed_one = normed_full.astype(jnp.bfloat16)
    packed = project(normed_one, packed_weight).astype(jnp.bfloat16)
    query_part = packed[..., :model_width]
    key_part = packed[..., model_width : 2 * model_width]
    value_part = packed[..., 2 * model_width :]
    attended, logsum_one = self_forward(query_part, key_part, value_part, caption_lengths)
    after_self = inputs + project(attended, output_weight)
    normed_full_two, scaled_two, inverse_two = layer_norm(
        after_self, norm_gains[:, 1], norm_shifts[:, 1]
    )
    normed_two = normed_full_two.astype(jnp.bfloat16)
    image_pair = project(paired, pair_weight).astype(jnp.bfloat16)
    image_key = image_pair[..., :model_width]
    image_value = image_pair[..., model_width:]
    query_rows = project(normed_two, query_weight).astype(jnp.bfloat16)
    mixed_rows, logsum_two = cross_forward(query_rows, image_key, image_value)
    branch = project(mixed_rows, cross_weight).astype(jnp.bfloat16)
    after_cross = after_self + branch.astype(jnp.float32)
    normed_full_three, scaled_three, inverse_three = layer_norm(
        after_cross, norm_gains[:, 2], norm_shifts[:, 2]
    )
    normed_three = normed_full_three.astype(jnp.bfloat16)
    gate_rows = project(normed_three, expand_full)
    hidden = gelu_exact(gate_rows).astype(jnp.bfloat16)
    caption_out = jnp.where(
        live_rows[..., None], after_cross + project(hidden, reduce_full), 0.0
    ).astype(jnp.bfloat16)

    grad_out = jnp.where(live_rows[..., None], cotangent, jnp.zeros_like(cotangent))
    reduce_grad = scatter_rows(weight_grad(hidden, grad_out).astype(jnp.bfloat16), True)
    _, gelu_pull = jax.vjp(gelu_exact, gate_rows)
    grad_gate = gelu_pull(project_back(grad_out, reduce_full))[0].astype(jnp.bfloat16)
    expand_grad = scatter_rows(weight_grad(normed_three, grad_gate).astype(jnp.bfloat16), False)
    grad_norm_three, gain_three, shift_three = norm_back(
        project_back(grad_gate, expand_full), scaled_three, inverse_three, norm_gains[:, 2]
    )
    grad_second = grad_out.astype(jnp.float32) + grad_norm_three
    grad_branch = grad_second.astype(jnp.bfloat16)
    cross_output_grad = weight_grad(mixed_rows, grad_branch)
    grad_cross_mixed = project_back(grad_branch, cross_weight).astype(jnp.bfloat16)
    grad_cross_rows, grad_image_key, grad_image_value = cross_backward(
        query_rows, image_key, image_value, logsum_two, grad_cross_mixed
    )
    grad_pair = jnp.concatenate([grad_image_key, grad_image_value], axis=-1)
    cross_pair_grad = weight_grad(paired, grad_pair)
    image_grad = route(
        project_back(grad_pair, pair_weight).astype(jnp.bfloat16), held, home_place
    )
    cross_query_grad = weight_grad(normed_two, grad_cross_rows)
    cross_sums = scatter_rows(
        jnp.concatenate([cross_pair_grad, cross_query_grad, cross_output_grad], axis=1).astype(
            jnp.bfloat16
        ),
        True,
    )
    grad_norm_two, gain_two, shift_two = norm_back(
        project_back(grad_cross_rows, query_weight).astype(jnp.bfloat16).astype(jnp.float32),
        scaled_two,
        inverse_two,
        norm_gains[:, 1],
    )
    grad_first = grad_second + grad_norm_two
    grad_self = grad_first.astype(jnp.bfloat16)
    self_output_grad = weight_grad(attended, grad_self)
    grad_attended = project_back(grad_self, output_weight).astype(jnp.bfloat16)
    grad_query, grad_key, grad_value = self_backward(
        query_part, key_part, value_part, caption_lengths, logsum_one, grad_attended
    )
    grad_packed = jnp.concatenate([grad_query, grad_key, grad_value], axis=-1)
    self_packed_grad = weight_grad(normed_one, grad_packed)
    grad_norm_one, gain_one, shift_one = norm_back(
        project_back(grad_packed, packed_weight), scaled_one, inverse_one, norm_gains[:, 0]
    )
    caption_grad = (grad_first + grad_norm_one).astype(jnp.bfloat16)
    norm_sums = jnp.stack([gain_one, gain_two, gain_three, shift_one, shift_two, shift_three], axis=1)
    self_sums = scatter_rows(
        jnp.concatenate(
            [self_packed_grad, self_output_grad, jnp.pad(norm_sums, ((0, 0), (0, 122)))], axis=1
        ).astype(jnp.bfloat16),
        False,
    )
    widen = lambda member: member.astype(jnp.float32)
    cross_sums, self_sums = widen(cross_sums), widen(self_sums)
    return (
        caption_out,
        caption_grad,
        image_grad,
        self_sums[:, 4 * model_width : 4 * model_width + 3],
        self_sums[:, 4 * model_width + 3 : 4 * model_width + 6],
        self_sums[:, : 3 * model_width],
        self_sums[:, 3 * model_width : 4 * model_width],
        cross_sums[:, 2 * model_width : 3 * model_width],
        cross_sums[:, : 2 * model_width],
        cross_sums[:, 3 * model_width :],
        widen(expand_grad),
        widen(reduce_grad),
    )


def solution(mesh):
    placed = (
        P(("dp", "seq"), None, None),
        P(("dp", "seq"), None, None),
        P(("dp", "seq")),
        P("dp"),
        P(("dp", "seq"), None),
        P(("dp", "seq"), None),
        P(("dp", "seq"), None),
        P(("dp", "seq"), None),
        P(("dp", "seq"), None),
        P(("dp", "seq"), None),
        P(("dp", "seq"), None),
        P(("dp", "seq"), None),
        P(("dp", "seq"), None),
        P(("dp", "seq"), None, None),
    )
    return jax.shard_map(
        shards,
        mesh=mesh,
        in_specs=placed,
        out_specs=(
            P(("dp", "seq"), None, None),
            P(("dp", "seq"), None, None),
            P(("dp", "seq"), None, None),
            P(("dp", "seq"), None),
            P(("dp", "seq"), None),
            P(("dp", "seq"), None),
            P(("dp", "seq"), None),
            P(("dp", "seq"), None),
            P(("dp", "seq"), None),
            P(("dp", "seq"), None),
            P(("dp", "seq"), None),
            P(("dp", "seq"), None),
        ),
        check_vma=False,
    )
```

time: 1560 us -> 555 us (0.36)
  waiting for transfers between devices: 1120 us -> 201 us
  blocking collectives: 115 us -> 0 us
  starting transfers between devices: 9.18 us -> 43.9 us
  matrix products: 134 us -> 102 us
  other arithmetic: 67.7 us -> 97 us
    reduce_scatter x12 -> x0, waiting for transfers between devices: 635 us -> none  [the longest x1 163 us: shards(): lax.psum_scatter(expand_grad, 'dp', scatter_dimension=0, tiled=True)]
    unnamed x27 -> x0, waiting for transfers between devices: 241 us -> none
    all_gather x7 -> x0, waiting for transfers between devices: 235 us -> none  [the longest x1 43.9 us: shards(): lax.all_gather(self_output, ('dp', 'seq'), axis=0, tiled=True)]
    ppermute x0 -> x46, waiting for transfers between devices: none -> 201 us  [the longest x20 116 us: scatter_rows(): state = kept + lax.ppermute(given, place[0], swap_pairs(*place))]
    all_gather x2 -> x0, blocking collectives: 80.2 us -> none  [the longest x1 43.5 us: shards(): lax.all_gather(norm_gain, ('dp', 'seq'), axis=0, tiled=True)]
    ppermute x0 -> x46, starting transfers between devices: none -> 43.9 us  [the longest x20 24.8 us: gather_rows(): other = lax.ppermute(state, place[0], swap_pairs(*place))]
    select_n x8 -> x30, other arithmetic: 4.4 us -> 38.3 us  [the longest x20 36.2 us: gather_rows(): jnp.where(own_bit(*place) == 0, jnp.concatenate([state, other], dim), jnp...]
    all_to_all x2 -> x0, blocking collectives: 29.2 us -> none  [the longest x1 14.8 us: shards(): lax.all_to_all(project_back(grad_cross_rows, query_back).astype(jnp.bfloa...]
  transfers between devices with their start and end apart: 25 -> 46, of which waited for: 21 -> 21; matrix products, arithmetic and copies ran while one was open for 15% -> 24% of each run, Pallas kernels for 0% -> 0%
where the time goes in v1:
time: 555 us; the launch traced here: 545 us
  waiting for transfers between devices  201 us (36%)
  matrix products  102 us (18%)
  other arithmetic  97 us (17%)
  local copies, waits for them, and re-layouts  83.7 us (15%)
  starting transfers between devices  43.9 us (8%)
  between operations  18.1 us (3%)
    ppermute x20, waiting for transfers between devices, scatter_rows(): state = kept + lax.ppermute(given, place[0], swap_pairs(*place))  116 us
    ppermute x20, waiting for transfers between devices, gather_rows(): other = lax.ppermute(state, place[0], swap_pairs(*place))  85 us
    select_n x20, other arithmetic, gather_rows(): jnp.where(own_bit(*place) == 0, jnp.concatenate([state, other], dim), jnp...  36.2 us
    dot_general x7, matrix products, project_back(): lax.dot_general(flat_rows, weight, (((1,), (1,)), ((), ())), preferred_el...  32.2 us
    unnamed x177, local copies, waits for them, and re-layouts  27.8 us
    ppermute x20, starting transfers between devices, gather_rows(): other = lax.ppermute(state, place[0], swap_pairs(*place))  24.8 us
    dot_general x7, matrix products, weight_grad(): lax.dot_general(left_rows.reshape(-1, left_rows.shape[-1]), right_rows.re...  21.5 us
    dot_general x7, matrix products, project(): jnp.dot(flat_rows, weight, preferred_element_type=jnp.float32)  20 us
  transfers between devices with their start and end apart: 46, of which 21 were waited for; matrix products, arithmetic and copies ran while one was open for 24% of the time, Pallas kernels for 0%

profile of v1, /device:TPU:0, one launch (start us, length us, event | category | flops | bytes accessed | tf_op | source)
XLA Modules:
  0.0 545.2 jit_solution(1372612134204304255)
XLA Ops:
  25.0 3.3 constant_dynamic-slice_fusion.3
  69.8 18.5 %collective-permute-done.1 = bf16[1,2,1,1,1,24,2432]{6,5,4,3,2,1,0:T(8,128)(2,1)S(1)} collective-permute-done((bf16[1,2,1,1,1,24,2432]{6,5,4,3,2,1,0:T(8,128)(2,1)}, bf16[1,2,1,1,1,24,2432]{6,5,4,3,2,1,0:T(8,128)(2,1)S(1)}, u32[]{:S(2)}, u32[]{:S(2)}) %collective-permute-start.1) | collective-permute-done | bytes 233504 | tf_op jit(solution)/shard_map/ppermute | solution.py:198
  96.5 4.4 collective-permute-done.19
  103.2 4.7 collective-permute-done.6
  119.4 13.7 %collective-permute-done.7 = bf16[2,2,1,1,1,24,3840]{6,5,4,3,2,1,0:T(8,128)(2,1)S(1)} collective-permute-done((bf16[2,2,1,1,1,24,3840]{6,5,4,3,2,1,0:T(8,128)(2,1)S(1)}, bf16[2,2,1,1,1,24,3840]{6,5,4,3,2,1,0:T(8,128)(2,1)S(1)}, u32[]{:S(2)}, u32[]{:S(2)}) %collective-permute-start.7) | collective-permute-done | bytes 737312 | tf_op jit(solution)/shard_map/ppermute | solution.py:198
  135.3 17.9 %collective-permute-done.3 = bf16[2,2,2,1,1,24,2432]{6,5,4,3,2,1,0:T(8,128)(2,1)S(1)} collective-permute-done((bf16[2,2,2,1,1,24,2432]{6,5,4,3,2,1,0:T(8,128)(2,1)S(1)}, bf16[2,2,2,1,1,24,2432]{6,5,4,3,2,1,0:T(8,128)(2,1)S(1)}, u32[]{:S(2)}, u32[]{:S(2)}) %collective-permute-start.3) | collective-permute-done | bytes 933920 | tf_op jit(solution)/shard_map/ppermute | solution.py:198
  156.5 19.1 %collective-permute-done.16 = bf16[2,2,2,1,1,24,3072]{6,5,4,3,2,1,0:T(8,128)(2,1)S(1)} collective-permute-done((bf16[2,2,2,1,1,24,3072]{6,5,4,3,2,1,0:T(8,128)(2,1)S(1)}, bf16[2,2,2,1,1,24,3072]{6,5,4,3,2,1,0:T(8,128)(2,1)S(1)}, u32[]{:S(2)}, u32[]{:S(2)}) %collective-permute-start.16) | collective-permute-done | bytes 1179680 | tf_op jit(solution)/shard_map/ppermute | solution.py:198
  193.1 6.8 %maximum_select_fusion.2 = bf16[2,2,2,2,2,96,768]{6,5,4,3,2,1,0:T(8,128)(2,1)} fusion(bf16[2,2,2,2,1,96,768]{6,5,4,3,2,1,0:T(8,128)(2,1)} %collective-permute-done.22, bf16[2,2,2,2,1,96,768]{6,5,4,3,2,1,0:T(8,128)(2,1)} %maximum_select_fusion.6, pred[]{:T(512)S(6)} %eq.13), kind=kLoop, calls=%fused_computation.37 | loop fusion | flops 7077888 | bytes 9437185 | tf_op jit(solution)/shard_map/jit(_where)/select_n | solution.py:199
  199.9 6.8 %maximum_select_fusion.1 = bf16[2,2,2,2,2,24,3072]{6,5,4,3,2,1,0:T(8,128)(2,1)} fusion(bf16[2,2,2,2,1,24,3072]{6,5,4,3,2,1,0:T(8,128)(2,1)} %collective-permute-done.17, bf16[2,2,2,2,1,24,3072]{6,5,4,3,2,1,0:T(8,128)(2,1)} %maximum_select_fusion.5, pred[]{:T(512)S(6)} %eq.13), kind=kLoop, calls=%fused_computation.36 | loop fusion | flops 7077888 | bytes 9437185 | tf_op jit(solution)/shard_map/jit(_where)/select_n | solution.py:199
  206.8 5.2 maximum_select_fusion
  241.2 4.3 fusion.50
  245.6 15.0 %multiply_convert_fusion = (bf16[4,128,3072]{2,1,0:T(8,128)(2,1)}, f32[4,128,3072]{2,1,0:T(8,128)S(1)}) fusion(f32[4,128,3072]{2,1,0:T(8,128)S(1)} %get-tuple-element.162, u8[128,3072]{1,0:T(8,128)(4,1)S(1)} %get-tuple-element.80, u8[128,3072]{1,0:T(8,128)(4,1)S(1)} %get-tuple-element.79), kind=kLoop, calls=%fused_computation.16 | loop fusion | flops 110100480 | bytes 16515072 | tf_op jit(solution)/shard_map/convert_element_type | solution.py:308
  260.6 8.4 %add_convert_fusion = bf16[4,128,3072]{2,1,0:T(8,128)(2,1)} fusion(f32[4,128,3072]{2,1,0:T(8,128)S(1)} %get-tuple-element.97, f32[4,128,3072]{2,1,0:T(8,128)S(1)} %get-tuple-element.162, bf16[3072,768,1]{1,0,2:T(8,128)(2,1)} %bitcast.393, bf16[4,128,768]{2,1,0:T(8,128)(2,1)} %param.31, pred[4,128]{1,0:T(4,128)(4,1)S(1)} %iota_compare_fusion.2), kind=kOutput, calls=%fused_computation.15 | convolution fusion | flops 2438332416 | bytes 21234176 | tf_op jit(solution)/shard_map/dot_general | solution.py:28
  269.0 6.7 %bitcast_convert_fusion.1 = bf16[768,3072]{1,0:T(8,128)(2,1)} fusion(bf16[4,128,3072]{2,1,0:T(8,128)(2,1)} %add_convert_fusion, f32[4,128,768]{2,1,0:T(8,128)S(1)} %subtract_multiply_fusion, f32[768]{0:T(1024)S(1)} %get-tuple-element.91, f32[768]{0:T(1024)S(1)} %get-tuple-element.90), kind=kOutput, calls=%fused_computation.7 | convolution fusion | flops 2419458048 | bytes 9443328 | tf_op jit(solution)/shard_map/dot_general | solution.py:35
  275.7 5.2 fusion.124
  289.2 5.7 %fusion.35 = bf16[4,12,64,196]{3,2,1,0:T(8,128)(2,1)} fusion(bf16[4,128,12,64]{1,3,2,0:T(8,128)(2,1)} %bitcast.359, f32[4,12,128,196]{2,3,1,0:T(8,128)} %copy-done, f32[4,12,128]{2,1,0:T(8,128)S(1)} %log_add_fusion.1), kind=kOutput, calls=%fused_computation.97 | convolution fusion | flops 158355456 | bytes 6832128 | tf_op jit(solution)/shard_map/bhqk,bqhe->bkhe/dot_general | solution.py:109
  294.8 4.1 multiply_reduce_fusion
  310.2 5.7 %fusion.52 = bf16[4,196,768]{2,1,0:T(8,128)(2,1)} fusion(bf16[768,3840]{1,0:T(8,128)(2,1)} %bitcast.354, bf16[4,196,768]{2,1,0:T(8,128)(2,1)} %copy.280, bf16[4,196,768]{2,1,0:T(8,128)(2,1)} %copy.279), kind=kOutput, calls=%fused_computation.129 | convolution fusion | flops 1855107072 | bytes 6021120 | tf_op jit(solution)/shard_map/dot_general | solution.py:28
  316.0 4.4 bitcast_convert_fusion.3
  366.3 4.6 fusion.9
  373.9 3.7 bitcast_convert_fusion.2
  389.2 3.5 select_convert_fusion
  413.0 17.4 %collective-permute-done.37 = bf16[2,2,2,1,1,24,3072]{6,5,4,3,2,1,0:T(8,128)(2,1)S(1)} collective-permute-done((bf16[2,2,2,1,1,24,3072]{6,5,4,3,2,1,0:T(8,128)(2,1)S(1)}, bf16[2,2,2,1,1,24,3072]{6,5,4,3,2,1,0:T(8,128)(2,1)S(1)}, u32[]{:S(2)}, u32[]{:S(2)}) %collective-permute-start.37) | collective-permute-done | bytes 1179680 | tf_op jit(solution)/shard_map/ppermute | solution.py:217
  435.2 24.0 %collective-permute-done.32 = bf16[2,2,1,2,1,24,3072]{6,5,4,3,2,1,0:T(8,128)(2,1)S(1)} collective-permute-done((bf16[2,2,1,2,1,24,3072]{6,5,4,3,2,1,0:T(8,128)(2,1)S(1)}, bf16[2,2,1,2,1,24,3072]{6,5,4,3,2,1,0:T(8,128)(2,1)S(1)}, u32[]{:S(2)}, u32[]{:S(2)}) %collective-permute-start.32) | collective-permute-done | bytes 1179680 | tf_op jit(solution)/shard_map/ppermute | solution.py:217
  462.1 9.7 %collective-permute-done.38 = bf16[2,2,1,1,1,24,3072]{6,5,4,3,2,1,0:T(8,128)(2,1)S(1)} collective-permute-done((bf16[2,2,1,1,1,24,3072]{6,5,4,3,2,1,0:T(8,128)(2,1)S(1)}, bf16[2,2,1,1,1,24,3072]{6,5,4,3,2,1,0:T(8,128)(2,1)S(1)}, u32[]{:S(2)}, u32[]{:S(2)}) %collective-permute-start.38) | collective-permute-done | bytes 589856 | tf_op jit(solution)/shard_map/ppermute | solution.py:217
  475.1 6.3 %collective-permute-done.33 = bf16[2,2,1,1,1,24,3072]{6,5,4,3,2,1,0:T(8,128)(2,1)S(1)} collective-permute-done((bf16[2,2,1,1,1,24,3072]{6,5,4,3,2,1,0:T(8,128)(2,1)S(1)}, bf16[2,2,1,1,1,24,3072]{6,5,4,3,2,1,0:T(8,128)(2,1)S(1)}, u32[]{:S(2)}, u32[]{:S(2)}) %collective-permute-start.33) | collective-permute-done | bytes 589856 | tf_op jit(solution)/shard_map/ppermute | solution.py:217
  484.6 23.0 %collective-permute-done.39 = bf16[1,2,1,1,1,24,3072]{6,5,4,3,2,1,0:T(8,128)(2,1)S(1)} collective-permute-done((bf16[1,2,1,1,1,24,3072]{6,5,4,3,2,1,0:T(8,128)(2,1)S(1)}, bf16[1,2,1,1,1,24,3072]{6,5,4,3,2,1,0:T(8,128)(2,1)S(1)}, u32[]{:S(2)}, u32[]{:S(2)}) %collective-permute-start.39) | collective-permute-done | bytes 294944 | tf_op jit(solution)/shard_map/ppermute | solution.py:217
  507.7 6.2 %collective-permute-done.44 = bf16[1,2,1,1,1,96,768]{6,5,4,3,2,1,0:T(8,128)(2,1)S(1)} collective-permute-done((bf16[1,2,1,1,1,96,768]{6,5,4,3,2,1,0:T(8,128)(2,1)S(1)}, bf16[1,2,1,1,1,96,768]{6,5,4,3,2,1,0:T(8,128)(2,1)S(1)}, u32[]{:S(2)}, u32[]{:S(2)}) %collective-permute-start.44) | collective-permute-done | bytes 294944 | tf_op jit(solution)/shard_map/ppermute | solution.py:217
  514.1 6.2 %collective-permute-done.34 = bf16[1,2,1,1,1,24,3072]{6,5,4,3,2,1,0:T(8,128)(2,1)S(1)} collective-permute-done((bf16[1,2,1,1,1,24,3072]{6,5,4,3,2,1,0:T(8,128)(2,1)S(1)}, bf16[1,2,1,1,1,24,3072]{6,5,4,3,2,1,0:T(8,128)(2,1)S(1)}, u32[]{:S(2)}, u32[]{:S(2)}) %collective-permute-start.34) | collective-permute-done | bytes 294944 | tf_op jit(solution)/shard_map/ppermute | solution.py:217
  520.4 7.8 %collective-permute-done.40 = bf16[1,1,1,1,1,24,3072]{6,5,4,3,2,1,0:T(8,128)(2,1)S(1)} collective-permute-done((bf16[1,1,1,1,1,24,3072]{6,5,4,3,2,1,0:T(8,128)(2,1)S(1)}, bf16[1,1,1,1,1,24,3072]{6,5,4,3,2,1,0:T(8,128)(2,1)S(1)}, u32[]{:S(2)}, u32[]{:S(2)}) %collective-permute-start.40) | collective-permute-done | bytes 147488 | tf_op jit(solution)/shard_map/ppermute | solution.py:217
  529.0 5.5 %collective-permute-done.35 = bf16[1,1,1,1,1,24,3072]{6,5,4,3,2,1,0:T(8,128)(2,1)S(1)} collective-permute-done((bf16[1,1,1,1,1,24,3072]{6,5,4,3,2,1,0:T(8,128)(2,1)S(1)}, bf16[1,1,1,1,1,24,3072]{6,5,4,3,2,1,0:T(8,128)(2,1)S(1)}, u32[]{:S(2)}, u32[]{:S(2)}) %collective-permute-start.35) | collective-permute-done | bytes 147488 | tf_op jit(solution)/shard_map/ppermute | solution.py:217
  536.7 5.2 collective-permute-done.30
  (465 shorter events, 244.0 us)
Async XLA Ops:
  0.7 48.6 %collective-permute-start.13 = (bf16[1,1,1,1,1,24,3072]{6,5,4,3,2,1,0:T(8,128)(2,1)}, bf16[1,1,1,1,1,24,3072]{6,5,4,3,2,1,0:T(8,128)(2,1)}, u32[]{:S(2)}, u32[]{:S(2)}) collective-permute-start(bf16[1,1,1,1,1,24,3072]{6,5,4,3,2,1,0:T(8,128)(2,1)} %bitcast.432), channel_id=1, source_target_pairs={{0,8},{4,12},{8,0},{12,4},{16,24},{20,28},{24,16},{28,20},{1,9},{5... | collective-permute-start | bytes 442376 | tf_op jit(solution)/shard_map/ppermute | solution.py:198
  3.8 49.3 %collective-permute-start.18 = (bf16[1,1,1,1,1,96,768]{6,5,4,3,2,1,0:T(8,128)(2,1)}, bf16[1,1,1,1,1,96,768]{6,5,4,3,2,1,0:T(8,128)(2,1)}, u32[]{:S(2)}, u32[]{:S(2)}) collective-permute-start(bf16[1,1,1,1,1,96,768]{6,5,4,3,2,1,0:T(8,128)(2,1)} %bitcast.435), channel_id=1, source_target_pairs={{0,8},{4,12},{8,0},{12,4},{16,24},{20,28},{24,16},{28,20},{1,9},{5... | collective-permute-start | bytes 442376 | tf_op jit(solution)/shard_map/ppermute | solution.py:198
  9.5 50.2 %collective-permute-start.5 = (bf16[1,1,1,1,1,24,3840]{6,5,4,3,2,1,0:T(8,128)(2,1)}, bf16[1,1,1,1,1,24,3840]{6,5,4,3,2,1,0:T(8,128)(2,1)}, u32[]{:S(2)}, u32[]{:S(2)}) collective-permute-start(bf16[1,1,1,1,1,24,3840]{6,5,4,3,2,1,0:T(8,128)(2,1)} %bitcast.23), channel_id=1, source_target_pairs={{0,8},{4,12},{8,0},{12,4},{16,24},{20,28},{24,16},{28,20},{1,9},{5... | collective-permute-start | bytes 552968 | tf_op jit(solution)/shard_map/ppermute | solution.py:198
  13.9 29.7 %collective-permute-start = (bf16[1,1,1,1,1,24,2432]{6,5,4,3,2,1,0:T(8,128)(2,1)}, bf16[1,1,1,1,1,24,2432]{6,5,4,3,2,1,0:T(8,128)(2,1)}, u32[]{:S(2)}, u32[]{:S(2)}) collective-permute-start(bf16[1,1,1,1,1,24,2432]{6,5,4,3,2,1,0:T(8,128)(2,1)} %get-tuple-element.142), channel_id=1, source_target_pairs={{0,8},{4,12},{8,0},{12,4},{16,24},{20,28},{24,16},{28,20},{1,9},{5... | collective-permute-start | bytes 350216 | tf_op jit(solution)/shard_map/ppermute | solution.py:198
  28.4 35.6 %collective-permute-start.12 = (bf16[1,196,768]{2,1,0:T(8,128)(2,1)S(1)}, bf16[1,196,768]{2,1,0:T(8,128)(2,1)}, u32[]{:S(2)}, u32[]{:S(2)}) collective-permute-start(bf16[1,196,768]{2,1,0:T(8,128)(2,1)S(1)} %copy_select_fusion), channel_id=1, source_target_pairs={{0,3},{1,2},{2,1},{3,0},{4,7},{5,6},{6,5},{7,4},{8,11},{9,10},{10,... | collective-permute-start | bytes 903176 | tf_op jit(solution)/shard_map/ppermute | solution.py:228
  53.1 35.3 %collective-permute-start.1 = (bf16[1,2,1,1,1,24,2432]{6,5,4,3,2,1,0:T(8,128)(2,1)}, bf16[1,2,1,1,1,24,2432]{6,5,4,3,2,1,0:T(8,128)(2,1)S(1)}, u32[]{:S(2)}, u32[]{:S(2)}) collective-permute-start(bf16[1,2,1,1,1,24,2432]{6,5,4,3,2,1,0:T(8,128)(2,1)} %maximum_select_fusion.27), channel_id=1, source_target_pairs={{0,16},{4,20},{8,24},{12,28},{16,0},{20,4},{24,8},{28,12},{1,17},{... | collective-permute-start | bytes 700424 | tf_op jit(solution)/shard_map/ppermute | solution.py:198
  59.8 34.9 %collective-permute-start.14 = (bf16[1,2,1,1,1,24,3072]{6,5,4,3,2,1,0:T(8,128)(2,1)}, bf16[1,2,1,1,1,24,3072]{6,5,4,3,2,1,0:T(8,128)(2,1)S(1)}, u32[]{:S(2)}, u32[]{:S(2)}) collective-permute-start(bf16[1,2,1,1,1,24,3072]{6,5,4,3,2,1,0:T(8,128)(2,1)} %maximum_select_fusion.23), channel_id=1, source_target_pairs={{0,16},{4,20},{8,24},{12,28},{16,0},{20,4},{24,8},{28,12},{1,17},{... | collective-permute-start | bytes 884744 | tf_op jit(solution)/shard_map/ppermute | solution.py:198
  64.0 36.9 %collective-permute-start.19 = (bf16[1,2,1,1,1,96,768]{6,5,4,3,2,1,0:T(8,128)(2,1)}, bf16[1,2,1,1,1,96,768]{6,5,4,3,2,1,0:T(8,128)(2,1)S(1)}, u32[]{:S(2)}, u32[]{:S(2)}) collective-permute-start(bf16[1,2,1,1,1,96,768]{6,5,4,3,2,1,0:T(8,128)(2,1)} %maximum_select_fusion.25), channel_id=1, source_target_pairs={{0,16},{4,20},{8,24},{12,28},{16,0},{20,4},{24,8},{28,12},{1,17},{... | collective-permute-start | bytes 884744 | tf_op jit(solution)/shard_map/ppermute | solution.py:198
  67.0 41.0 %collective-permute-start.6 = (bf16[1,2,1,1,1,24,3840]{6,5,4,3,2,1,0:T(8,128)(2,1)}, bf16[1,2,1,1,1,24,3840]{6,5,4,3,2,1,0:T(8,128)(2,1)S(1)}, u32[]{:S(2)}, u32[]{:S(2)}) collective-permute-start(bf16[1,2,1,1,1,24,3840]{6,5,4,3,2,1,0:T(8,128)(2,1)} %maximum_select_fusion.21), channel_id=1, source_target_pairs={{0,16},{4,20},{8,24},{12,28},{16,0},{20,4},{24,8},{28,12},{1,17},{... | collective-permute-start | bytes 1105928 | tf_op jit(solution)/shard_map/ppermute | solution.py:198
  108.1 25.1 %collective-permute-start.7 = (bf16[2,2,1,1,1,24,3840]{6,5,4,3,2,1,0:T(8,128)(2,1)S(1)}, bf16[2,2,1,1,1,24,3840]{6,5,4,3,2,1,0:T(8,128)(2,1)S(1)}, u32[]{:S(2)}, u32[]{:S(2)}) collective-permute-start(bf16[2,2,1,1,1,24,3840]{6,5,4,3,2,1,0:T(8,128)(2,1)S(1)} %fusion.70), channel_id=1, source_target_pairs={{0,2},{1,3},{2,0},{3,1},{4,6},{5,7},{6,4},{7,5},{8,10},{9,11},{10,... | collective-permute-start | bytes 2211848 | tf_op jit(solution)/shard_map/ppermute | solution.py:198
  110.2 43.0 %collective-permute-start.3 = (bf16[2,2,2,1,1,24,2432]{6,5,4,3,2,1,0:T(8,128)(2,1)S(1)}, bf16[2,2,2,1,1,24,2432]{6,5,4,3,2,1,0:T(8,128)(2,1)S(1)}, u32[]{:S(2)}, u32[]{:S(2)}) collective-permute-start(bf16[2,2,2,1,1,24,2432]{6,5,4,3,2,1,0:T(8,128)(2,1)S(1)} %maximum_select_fusion.15), channel_id=1, source_target_pairs={{0,2},{1,3},{2,0},{3,1},{4,6},{5,7},{6,4},{7,5},{8,10},{9,11},{10,... | collective-permute-start | bytes 2801672 | tf_op jit(solution)/shard_map/ppermute | solution.py:198
  113.5 62.2 %collective-permute-start.16 = (bf16[2,2,2,1,1,24,3072]{6,5,4,3,2,1,0:T(8,128)(2,1)S(1)}, bf16[2,2,2,1,1,24,3072]{6,5,4,3,2,1,0:T(8,128)(2,1)S(1)}, u32[]{:S(2)}, u32[]{:S(2)}) collective-permute-start(bf16[2,2,2,1,1,24,3072]{6,5,4,3,2,1,0:T(8,128)(2,1)S(1)} %maximum_select_fusion.11), channel_id=1, source_target_pairs={{0,2},{1,3},{2,0},{3,1},{4,6},{5,7},{6,4},{7,5},{8,10},{9,11},{10,... | collective-permute-start | bytes 3538952 | tf_op jit(solution)/shard_map/ppermute | solution.py:198
  117.7 36.6 %collective-permute-start.21 = (bf16[2,2,1,2,1,96,768]{6,5,4,3,2,1,0:T(8,128)(2,1)S(1)}, bf16[2,2,1,2,1,96,768]{6,5,4,3,2,1,0:T(8,128)(2,1)S(1)}, u32[]{:S(2)}, u32[]{:S(2)}) collective-permute-start(bf16[2,2,1,2,1,96,768]{6,5,4,3,2,1,0:T(8,128)(2,1)S(1)} %maximum_select_fusion.13), channel_id=1, source_target_pairs={{0,4},{4,0},{8,12},{12,8},{16,20},{20,16},{24,28},{28,24},{1,5},{5... | collective-permute-start | bytes 3538952 | tf_op jit(solution)/shard_map/ppermute | solution.py:198
  133.5 43.8 %collective-permute-start.8 = (bf16[2,2,1,2,1,24,3840]{6,5,4,3,2,1,0:T(8,128)(2,1)S(1)}, bf16[2,2,1,2,1,24,3840]{6,5,4,3,2,1,0:T(8,128)(2,1)S(1)}, u32[]{:S(2)}, u32[]{:S(2)}) collective-permute-start(bf16[2,2,1,2,1,24,3840]{6,5,4,3,2,1,0:T(8,128)(2,1)S(1)} %maximum_select_fusion.9), channel_id=1, source_target_pairs={{0,4},{4,0},{8,12},{12,8},{16,20},{20,16},{24,28},{28,24},{1,5},{5... | collective-permute-start | bytes 4423688 | tf_op jit(solution)/shard_map/ppermute | solution.py:198
  153.7 26.4 %collective-permute-start.4 = (bf16[2,2,2,2,1,24,2432]{6,5,4,3,2,1,0:T(8,128)(2,1)S(1)}, bf16[2,2,2,2,1,24,2432]{6,5,4,3,2,1,0:T(8,128)(2,1)S(1)}, u32[]{:S(2)}, u32[]{:S(2)}) collective-permute-start(bf16[2,2,2,2,1,24,2432]{6,5,4,3,2,1,0:T(8,128)(2,1)S(1)} %maximum_select_fusion.7), channel_id=1, source_target_pairs={{0,1},{1,0},{2,3},{3,2},{4,5},{5,4},{6,7},{7,6},{8,9},{9,8},{10,11... | collective-permute-start | bytes 5603336 | tf_op jit(solution)/shard_map/ppermute | solution.py:198
  156.1 37.1 %collective-permute-start.22 = (bf16[2,2,2,2,1,96,768]{6,5,4,3,2,1,0:T(8,128)(2,1)}, bf16[2,2,2,2,1,96,768]{6,5,4,3,2,1,0:T(8,128)(2,1)}, u32[]{:S(2)}, u32[]{:S(2)}) collective-permute-start(bf16[2,2,2,2,1,96,768]{6,5,4,3,2,1,0:T(8,128)(2,1)} %maximum_select_fusion.6), channel_id=1, source_target_pairs={{0,1},{1,0},{2,3},{3,2},{4,5},{5,4},{6,7},{7,6},{8,9},{9,8},{10,11... | collective-permute-start | bytes 7077896 | tf_op jit(solution)/shard_map/ppermute | solution.py:198
  179.6 27.1 %collective-permute-start.9 = (bf16[2,2,2,2,1,24,3840]{6,5,4,3,2,1,0:T(8,128)(2,1)}, bf16[2,2,2,2,1,24,3840]{6,5,4,3,2,1,0:T(8,128)(2,1)}, u32[]{:S(2)}, u32[]{:S(2)}) collective-permute-start(bf16[2,2,2,2,1,24,3840]{6,5,4,3,2,1,0:T(8,128)(2,1)} %maximum_select_fusion.4), channel_id=1, source_target_pairs={{0,1},{1,0},{2,3},{3,2},{4,5},{5,4},{6,7},{7,6},{8,9},{9,8},{10,11... | collective-permute-start | bytes 8847368 | tf_op jit(solution)/shard_map/ppermute | solution.py:198
  349.0 49.5 %collective-permute-start.36 = (bf16[2,2,2,2,1,24,3072]{6,5,4,3,2,1,0:T(8,128)(2,1)}, bf16[2,2,2,2,1,24,3072]{6,5,4,3,2,1,0:T(8,128)(2,1)}, u32[]{:S(2)}, u32[]{:S(2)}) collective-permute-start(bf16[2,2,2,2,1,24,3072]{6,5,4,3,2,1,0:T(8,128)(2,1)} %constant_dynamic-slice_fusion.13), channel_id=1, source_target_pairs={{0,1},{1,0},{2,3},{3,2},{4,5},{5,4},{6,7},{7,6},{8,9},{9,8},{10,11... | collective-permute-start | bytes 7077896 | tf_op jit(solution)/shard_map/ppermute | solution.py:217
  349.0 54.0 %collective-permute-start.41 = (bf16[2,2,2,2,1,96,768]{6,5,4,3,2,1,0:T(8,128)(2,1)}, bf16[2,2,2,2,1,96,768]{6,5,4,3,2,1,0:T(8,128)(2,1)}, u32[]{:S(2)}, u32[]{:S(2)}) collective-permute-start(bf16[2,2,2,2,1,96,768]{6,5,4,3,2,1,0:T(8,128)(2,1)} %constant_dynamic-slice_fusion.8), channel_id=1, source_target_pairs={{0,1},{1,0},{2,3},{3,2},{4,5},{5,4},{6,7},{7,6},{8,9},{9,8},{10,11... | collective-permute-start | bytes 7077896 | tf_op jit(solution)/shard_map/ppermute | solution.py:217
  352.6 40.1 %collective-permute-start.25 = (bf16[1,196,768]{2,1,0:T(8,128)(2,1)}, bf16[1,196,768]{2,1,0:T(8,128)(2,1)}, u32[]{:S(2)}, u32[]{:S(2)}) collective-permute-start(bf16[1,196,768]{2,1,0:T(8,128)(2,1)} %get-tuple-element.105), channel_id=1, source_target_pairs={{0,3},{1,2},{2,1},{3,0},{4,7},{5,6},{6,5},{7,4},{8,11},{9,10},{10,... | collective-permute-start | bytes 903176 | tf_op jit(solution)/shard_map/ppermute | solution.py:228
  353.6 41.0 %collective-permute-start.24 = (bf16[1,196,768]{2,1,0:T(8,128)(2,1)}, bf16[1,196,768]{2,1,0:T(8,128)(2,1)}, u32[]{:S(2)}, u32[]{:S(2)}) collective-permute-start(bf16[1,196,768]{2,1,0:T(8,128)(2,1)} %get-tuple-element.106), channel_id=1, source_target_pairs={{0,2},{1,3},{2,0},{3,1},{4,6},{5,7},{6,4},{7,5},{8,10},{9,11},{10,... | collective-permute-start | bytes 903176 | tf_op jit(solution)/shard_map/ppermute | solution.py:228
  354.2 40.5 %collective-permute-start.23 = (bf16[1,196,768]{2,1,0:T(8,128)(2,1)}, bf16[1,196,768]{2,1,0:T(8,128)(2,1)}, u32[]{:S(2)}, u32[]{:S(2)}) collective-permute-start(bf16[1,196,768]{2,1,0:T(8,128)(2,1)} %get-tuple-element.107), channel_id=1, source_target_pairs={{0,1},{1,0},{2,3},{3,2},{4,5},{5,4},{6,7},{7,6},{8,9},{9,8},{10,11... | collective-permute-start | bytes 903176 | tf_op jit(solution)/shard_map/ppermute | solution.py:228
  401.5 28.9 %collective-permute-start.37 = (bf16[2,2,2,1,1,24,3072]{6,5,4,3,2,1,0:T(8,128)(2,1)S(1)}, bf16[2,2,2,1,1,24,3072]{6,5,4,3,2,1,0:T(8,128)(2,1)S(1)}, u32[]{:S(2)}, u32[]{:S(2)}) collective-permute-start(bf16[2,2,2,1,1,24,3072]{6,5,4,3,2,1,0:T(8,128)(2,1)S(1)} %constant_dynamic-slice_fusion.12), channel_id=1, source_target_pairs={{0,2},{1,3},{2,0},{3,1},{4,6},{5,7},{6,4},{7,5},{8,10},{9,11},{10,... | collective-permute-start | bytes 3538952 | tf_op jit(solution)/shard_map/ppermute | solution.py:217
  405.0 28.9 %collective-permute-start.42 = (bf16[2,2,1,2,1,96,768]{6,5,4,3,2,1,0:T(8,128)(2,1)S(1)}, bf16[2,2,1,2,1,96,768]{6,5,4,3,2,1,0:T(8,128)(2,1)S(1)}, u32[]{:S(2)}, u32[]{:S(2)}) collective-permute-start(bf16[2,2,1,2,1,96,768]{6,5,4,3,2,1,0:T(8,128)(2,1)S(1)} %constant_dynamic-slice_fusion.7), channel_id=1, source_target_pairs={{0,4},{4,0},{8,12},{12,8},{16,20},{20,16},{24,28},{28,24},{1,5},{5... | collective-permute-start | bytes 3538952 | tf_op jit(solution)/shard_map/ppermute | solution.py:217
  408.7 50.5 %collective-permute-start.32 = (bf16[2,2,1,2,1,24,3072]{6,5,4,3,2,1,0:T(8,128)(2,1)S(1)}, bf16[2,2,1,2,1,24,3072]{6,5,4,3,2,1,0:T(8,128)(2,1)S(1)}, u32[]{:S(2)}, u32[]{:S(2)}) collective-permute-start(bf16[2,2,1,2,1,24,3072]{6,5,4,3,2,1,0:T(8,128)(2,1)S(1)} %constant_dynamic-slice_fusion.17), channel_id=1, source_target_pairs={{0,4},{4,0},{8,12},{12,8},{16,20},{20,16},{24,28},{28,24},{1,5},{5... | collective-permute-start | bytes 3538952 | tf_op jit(solution)/shard_map/ppermute | solution.py:217
  411.8 48.7 %collective-permute-start.27 = (bf16[2,2,2,1,1,24,3200]{6,5,4,3,2,1,0:T(8,128)(2,1)S(1)}, bf16[2,2,2,1,1,24,3200]{6,5,4,3,2,1,0:T(8,128)(2,1)S(1)}, u32[]{:S(2)}, u32[]{:S(2)}) collective-permute-start(bf16[2,2,2,1,1,24,3200]{6,5,4,3,2,1,0:T(8,128)(2,1)S(1)} %constant_dynamic-slice_fusion.22), channel_id=1, source_target_pairs={{0,2},{1,3},{2,0},{3,1},{4,6},{5,7},{6,4},{7,5},{8,10},{9,11},{10,... | collective-permute-start | bytes 3686408 | tf_op jit(solution)/shard_map/ppermute | solution.py:217
  430.6 41.2 %collective-permute-start.38 = (bf16[2,2,1,1,1,24,3072]{6,5,4,3,2,1,0:T(8,128)(2,1)S(1)}, bf16[2,2,1,1,1,24,3072]{6,5,4,3,2,1,0:T(8,128)(2,1)S(1)}, u32[]{:S(2)}, u32[]{:S(2)}) collective-permute-start(bf16[2,2,1,1,1,24,3072]{6,5,4,3,2,1,0:T(8,128)(2,1)S(1)} %constant_dynamic-slice_fusion.11), channel_id=1, source_target_pairs={{0,4},{4,0},{8,12},{12,8},{16,20},{20,16},{24,28},{28,24},{1,5},{5... | collective-permute-start | bytes 1769480 | tf_op jit(solution)/shard_map/ppermute | solution.py:217
  434.1 37.9 %collective-permute-start.43 = (bf16[2,2,1,1,1,96,768]{6,5,4,3,2,1,0:T(8,128)(2,1)S(1)}, bf16[2,2,1,1,1,96,768]{6,5,4,3,2,1,0:T(8,128)(2,1)S(1)}, u32[]{:S(2)}, u32[]{:S(2)}) collective-permute-start(bf16[2,2,1,1,1,96,768]{6,5,4,3,2,1,0:T(8,128)(2,1)S(1)} %constant_dynamic-slice_fusion.6), channel_id=1, source_target_pairs={{0,2},{1,3},{2,0},{3,1},{4,6},{5,7},{6,4},{7,5},{8,10},{9,11},{10,... | collective-permute-start | bytes 1769480 | tf_op jit(solution)/shard_map/ppermute | solution.py:217
  471.9 35.7 %collective-permute-start.39 = (bf16[1,2,1,1,1,24,3072]{6,5,4,3,2,1,0:T(8,128)(2,1)S(1)}, bf16[1,2,1,1,1,24,3072]{6,5,4,3,2,1,0:T(8,128)(2,1)S(1)}, u32[]{:S(2)}, u32[]{:S(2)}) collective-permute-start(bf16[1,2,1,1,1,24,3072]{6,5,4,3,2,1,0:T(8,128)(2,1)S(1)} %constant_dynamic-slice_fusion.10), channel_id=1, source_target_pairs={{0,16},{4,20},{8,24},{12,28},{16,0},{20,4},{24,8},{28,12},{1,17},{... | collective-permute-start | bytes 884744 | tf_op jit(solution)/shard_map/ppermute | solution.py:217
  472.1 41.8 %collective-permute-start.44 = (bf16[1,2,1,1,1,96,768]{6,5,4,3,2,1,0:T(8,128)(2,1)S(1)}, bf16[1,2,1,1,1,96,768]{6,5,4,3,2,1,0:T(8,128)(2,1)S(1)}, u32[]{:S(2)}, u32[]{:S(2)}) collective-permute-start(bf16[1,2,1,1,1,96,768]{6,5,4,3,2,1,0:T(8,128)(2,1)S(1)} %constant_dynamic-slice_fusion.5), channel_id=1, source_target_pairs={{0,16},{4,20},{8,24},{12,28},{16,0},{20,4},{24,8},{28,12},{1,17},{... | collective-permute-start | bytes 884744 | tf_op jit(solution)/shard_map/ppermute | solution.py:217
  481.5 38.8 %collective-permute-start.34 = (bf16[1,2,1,1,1,24,3072]{6,5,4,3,2,1,0:T(8,128)(2,1)S(1)}, bf16[1,2,1,1,1,24,3072]{6,5,4,3,2,1,0:T(8,128)(2,1)S(1)}, u32[]{:S(2)}, u32[]{:S(2)}) collective-permute-start(bf16[1,2,1,1,1,24,3072]{6,5,4,3,2,1,0:T(8,128)(2,1)S(1)} %constant_dynamic-slice_fusion.15), channel_id=1, source_target_pairs={{0,16},{4,20},{8,24},{12,28},{16,0},{20,4},{24,8},{28,12},{1,17},{... | collective-permute-start | bytes 884744 | tf_op jit(solution)/shard_map/ppermute | solution.py:217
  484.3 51.7 %collective-permute-start.29 = (bf16[1,2,1,1,1,24,3200]{6,5,4,3,2,1,0:T(8,128)(2,1)S(1)}, bf16[1,2,1,1,1,24,3200]{6,5,4,3,2,1,0:T(8,128)(2,1)S(1)}, u32[]{:S(2)}, u32[]{:S(2)}) collective-permute-start(bf16[1,2,1,1,1,24,3200]{6,5,4,3,2,1,0:T(8,128)(2,1)S(1)} %constant_dynamic-slice_fusion.20), channel_id=1, source_target_pairs={{0,16},{4,20},{8,24},{12,28},{16,0},{20,4},{24,8},{28,12},{1,17},{... | collective-permute-start | bytes 921608 | tf_op jit(solution)/shard_map/ppermute | solution.py:217
  (97 other events, 766.4 us)

commit v2 on v1

--- a/solution.py
+++ b/solution.py
@@ -192,30 +192,52 @@
 
 def gather_rows(part, flip):
     bits = index_bits()
-    state = part.reshape((1,) * len(bits) + part.shape)
+    own = [own_bit(*place) for place in bits]
+    rest = [0] * part.ndim
+    known = [1] * len(bits)
+    piece = part.reshape((1,) * len(bits) + part.shape)
+    whole = jnp.zeros((2,) * len(bits) + part.shape, part.dtype)
+    whole = lax.dynamic_update_slice(whole, piece, own + rest)
     for place in gather_order(flip):
         dim = bits.index(place)
-        other = lax.ppermute(state, place[0], swap_pairs(*place))
-        state = jnp.where(
-            own_bit(*place) == 0,
-            jnp.concatenate([state, other], dim),
-            jnp.concatenate([other, state], dim),
-        )
-    return state.reshape((-1,) + part.shape[1:])
-
-
-def scatter_rows(whole, flip):
-    bits = index_bits()
-    rows = whole.shape[0] >> len(bits)
-    state = whole.reshape((2,) * len(bits) + (rows,) + whole.shape[1:])
-    order = gather_order(flip)
-    for place in [order[-1]] + order[:-1][::-1]:
-        dim = bits.index(place)
+        starts = [0 if size == 2 else bit for size, bit in zip(known, own)]
+        if max(known) == 2:
+            piece = lax.dynamic_slice(whole, starts + rest, known + list(part.shape))
+        other = lax.ppermute(piece, place[0], swap_pairs(*place))
+        starts[dim] = 1 - own[dim]
+        whole = lax.dynamic_update_slice(whole, other, starts + rest)
+        known[dim] = 2
+    return whole.reshape((-1,) + part.shape[1:])
+
+
+class Scatter:
+    def __init__(self, whole, flip):
+        bits = index_bits()
+        self.rows = whole.shape[0] >> len(bits)
+        self.tail = whole.shape[1:]
+        self.state = whole.reshape((2,) * len(bits) + (self.rows,) + self.tail)
+        order = gather_order(flip)
+        self.left = [order[-1]] + order[:-1][::-1]
+
+    def step(self):
+        place = self.left.pop(0)
+        dim = index_bits().index(place)
         mine = own_bit(*place)
-        given = lax.dynamic_slice_in_dim(state, 1 - mine, 1, dim)
-        kept = lax.dynamic_slice_in_dim(state, mine, 1, dim)
-        state = kept + lax.ppermute(given, place[0], swap_pairs(*place))
-    return state.reshape((rows,) + whole.shape[1:])
+        given = lax.dynamic_slice_in_dim(self.state, 1 - mine, 1, dim)
+        kept = lax.dynamic_slice_in_dim(self.state, mine, 1, dim)
+        self.state = kept + lax.ppermute(given, place[0], swap_pairs(*place))
+
+    def finish(self):
+        while self.left:
+            self.step()
+        return self.state.reshape((self.rows,) + self.tail).astype(jnp.float32)
+
+
+def tie(scatters, *values):
+    held = lax.optimization_barrier(tuple(one.state for one in scatters) + values)
+    for one, state in zip(scatters, held):
+        one.state = state
+    return held[len(scatters):] if len(values) > 1 else held[-1]
 
 
 def route(table_rows, pick, place):
@@ -266,18 +288,33 @@
 
     norm_columns = jnp.pad(jnp.concatenate([norm_gain, norm_bias], axis=1), ((0, 0), (0, 122)))
     first_group = gather_rows(jnp.concatenate([self_packed, norm_columns], axis=1), False)
-    second_group = gather_rows(
-        jnp.concatenate([cross_pair, self_output, cross_query, cross_output], axis=1), True
-    )
-    expand_full = gather_rows(expand_weight, False)
-    reduce_full = gather_rows(reduce_weight, True)
+    rows = self_packed.shape[0]
+    ratio = reduce_weight.shape[0] // rows
+    reduce_blocks = [reduce_weight[k * rows : (k + 1) * rows] for k in range(ratio)]
+    others = lax.all_gather(
+        jnp.concatenate(
+            [cross_pair, self_output, cross_query, cross_output, expand_weight] + reduce_blocks,
+            axis=1,
+        ),
+        ("dp", "seq"),
+        axis=0,
+        tiled=True,
+    )
     packed_weight = first_group[:, : 3 * model_width]
     norm_values = first_group[:, 3 * model_width : 3 * model_width + 6].astype(jnp.float32)
     norm_gains, norm_shifts = norm_values[:, :3], norm_values[:, 3:]
-    pair_weight = second_group[:, : 2 * model_width]
-    output_weight = second_group[:, 2 * model_width : 3 * model_width]
-    query_weight = second_group[:, 3 * model_width : 4 * model_width]
-    cross_weight = second_group[:, 4 * model_width :]
+    pair_weight = others[:, : 2 * model_width]
+    output_weight = others[:, 2 * model_width : 3 * model_width]
+    query_weight = others[:, 3 * model_width : 4 * model_width]
+    cross_weight = others[:, 4 * model_width : 5 * model_width]
+    hidden_width = expand_weight.shape[1]
+    expand_full = others[:, 5 * model_width : 5 * model_width + hidden_width]
+    reduce_full = (
+        others[:, 5 * model_width + hidden_width :]
+        .reshape(-1, rows, ratio, model_width)
+        .transpose(0, 2, 1, 3)
+        .reshape(-1, model_width)
+    )
 
     live_rows = jnp.arange(seq_len)[None, :] < caption_lengths[:, None]
     inputs = caption_tokens.astype(jnp.float32)
@@ -311,10 +348,16 @@
     ).astype(jnp.bfloat16)
 
     grad_out = jnp.where(live_rows[..., None], cotangent, jnp.zeros_like(cotangent))
-    reduce_grad = scatter_rows(weight_grad(hidden, grad_out).astype(jnp.bfloat16), True)
+    narrow = lambda member: member.astype(jnp.bfloat16)
+    reduce_sums = Scatter(narrow(weight_grad(hidden, grad_out)), True)
+    grad_late = tie([reduce_sums], grad_out)
+    reduce_sums.step()
     _, gelu_pull = jax.vjp(gelu_exact, gate_rows)
-    grad_gate = gelu_pull(project_back(grad_out, reduce_full))[0].astype(jnp.bfloat16)
-    expand_grad = scatter_rows(weight_grad(normed_three, grad_gate).astype(jnp.bfloat16), False)
+    grad_gate = gelu_pull(project_back(grad_late, reduce_full))[0].astype(jnp.bfloat16)
+    expand_sums = Scatter(narrow(weight_grad(normed_three, grad_gate)), False)
+    grad_gate = tie([reduce_sums, expand_sums], grad_gate)
+    reduce_sums.step()
+    expand_sums.step()
     grad_norm_three, gain_three, shift_three = norm_back(
         project_back(grad_gate, expand_full), scaled_three, inverse_three, norm_gains[:, 2]
     )
@@ -322,21 +365,20 @@
     grad_branch = grad_second.astype(jnp.bfloat16)
     cross_output_grad = weight_grad(mixed_rows, grad_branch)
     grad_cross_mixed = project_back(grad_branch, cross_weight).astype(jnp.bfloat16)
+    grad_cross_mixed = tie([expand_sums], grad_cross_mixed)
+    expand_sums.step()
     grad_cross_rows, grad_image_key, grad_image_value = cross_backward(
         query_rows, image_key, image_value, logsum_two, grad_cross_mixed
     )
     grad_pair = jnp.concatenate([grad_image_key, grad_image_value], axis=-1)
-    cross_pair_grad = weight_grad(paired, grad_pair)
+    grad_cross_rows, grad_pair = tie([reduce_sums, expand_sums], grad_cross_rows, grad_pair)
+    reduce_sums.step()
+    expand_sums.step()
     image_grad = route(
         project_back(grad_pair, pair_weight).astype(jnp.bfloat16), held, home_place
     )
+    cross_pair_grad = weight_grad(paired, grad_pair)
     cross_query_grad = weight_grad(normed_two, grad_cross_rows)
-    cross_sums = scatter_rows(
-        jnp.concatenate([cross_pair_grad, cross_query_grad, cross_output_grad], axis=1).astype(
-            jnp.bfloat16
-        ),
-        True,
-    )
     grad_norm_two, gain_two, shift_two = norm_back(
         project_back(grad_cross_rows, query_weight).astype(jnp.bfloat16).astype(jnp.float32),
         scaled_two,
@@ -346,38 +388,57 @@
     grad_first = grad_second + grad_norm_two
     grad_self = grad_first.astype(jnp.bfloat16)
     self_output_grad = weight_grad(attended, grad_self)
+    cross_sums = Scatter(
+        narrow(
+            jnp.concatenate(
+                [cross_pair_grad, cross_query_grad, cross_output_grad, self_output_grad], axis=1
+            )
+        ),
+        True,
+    )
+    grad_self = tie([reduce_sums, expand_sums, cross_sums], grad_self)
+    reduce_sums.step()
+    expand_sums.step()
+    cross_sums.step()
     grad_attended = project_back(grad_self, output_weight).astype(jnp.bfloat16)
     grad_query, grad_key, grad_value = self_backward(
         query_part, key_part, value_part, caption_lengths, logsum_one, grad_attended
     )
     grad_packed = jnp.concatenate([grad_query, grad_key, grad_value], axis=-1)
+    grad_packed = tie([reduce_sums, expand_sums, cross_sums], grad_packed)
+    cross_sums.step()
     self_packed_grad = weight_grad(normed_one, grad_packed)
     grad_norm_one, gain_one, shift_one = norm_back(
         project_back(grad_packed, packed_weight), scaled_one, inverse_one, norm_gains[:, 0]
     )
     caption_grad = (grad_first + grad_norm_one).astype(jnp.bfloat16)
     norm_sums = jnp.stack([gain_one, gain_two, gain_three, shift_one, shift_two, shift_three], axis=1)
-    self_sums = scatter_rows(
-        jnp.concatenate(
-            [self_packed_grad, self_output_grad, jnp.pad(norm_sums, ((0, 0), (0, 122)))], axis=1
-        ).astype(jnp.bfloat16),
-        False,
-    )
-    widen = lambda member: member.astype(jnp.float32)
-    cross_sums, self_sums = widen(cross_sums), widen(self_sums)
+    half = 3 * model_width // 2
+    first_sums = Scatter(narrow(self_packed_grad[:, :half]), False)
+    second_sums = Scatter(
+        narrow(
+            jnp.concatenate(
+                [self_packed_grad[:, half:], jnp.pad(norm_sums, ((0, 0), (0, 122)))], axis=1
+            )
+        ),
+        True,
+    )
+    reduce_grad, expand_grad = reduce_sums.finish(), expand_sums.finish()
+    first_sums, second_sums = first_sums.finish(), second_sums.finish()
+    cross_sums = cross_sums.finish()
     return (
         caption_out,
         caption_grad,
         image_grad,
-        self_sums[:, 4 * model_width : 4 * model_width + 3],
-        self_sums[:, 4 * model_width + 3 : 4 * model_width + 6],
-        self_sums[:, : 3 * model_width],
-        self_sums[:, 3 * model_width : 4 * model_width],
+        second_sums[:, half : half + 3],
+        second_sums[:, half + 3 : half + 6],
+        jnp.concatenate([first_sums, second_sums[:, :half]], axis=1),
+        cross_sums[:, 4 * model_width :],
         cross_sums[:, 2 * model_width : 3 * model_width],
         cross_sums[:, : 2 * model_width],
-        cross_sums[:, 3 * model_width :],
-        widen(expand_grad),
-        widen(reduce_grad),
+        cross_sums[:, 3 * model_width : 4 * model_width],
+        expand_grad,
+        reduce_grad,
     )
 
 

time: 555 us -> 540 us (0.973)
  waiting for transfers between devices: 201 us -> 168 us
  local copies, waits for them, and re-layouts: 83.7 us -> 116 us
  other arithmetic: 97 us -> 82.9 us
  starting transfers between devices: 43.9 us -> 30.1 us
  between operations: 18.1 us -> 31.2 us
    ppermute x40 -> x30, waiting for transfers between devices: 201 us -> 157 us  [the longest x25 86.9 us: step(): self.state = kept + lax.ppermute(given, place[0], swap_pairs(*place))]
    select_n x20 -> x1, other arithmetic: 36.2 us -> 1.02 us  [shards(): jnp.where(live_rows[..., None], cotangent, jnp.zeros_like(cotangent))]
    dynamic_slice x20 -> x28, local copies, waits for them, and re-layouts: 7.45 us -> 22.6 us  [the longest x24 15.1 us: step(): given = lax.dynamic_slice_in_dim(self.state, 1 - mine, 1, dim)]
    ppermute x40 -> x30, starting transfers between devices: 39.8 us -> 25.9 us  [the longest x25 18.5 us: step(): self.state = kept + lax.ppermute(given, place[0], swap_pairs(*place))]
    ppermute x6, waiting for transfers between devices: 0.02 us -> 11.2 us  [route(): rows = lax.ppermute(rows, 'seq', [(i, i ^ k) for i in range(peers)])]
    convert_element_type x1, other arithmetic: 15 us -> 26.2 us  [shards(): hidden = gelu_exact(gate_rows).astype(jnp.bfloat16)]
    reshape x0 -> x1, local copies, waits for them, and re-layouts: none -> 9.75 us  [shards(): reduce_full = others[:, 5 * model_width + hidden_width:].reshape(-1, rows...]
    dot_general x7, matrix products: 20 us -> 28.8 us  [project(): jnp.dot(flat_rows, weight, preferred_element_type=jnp.float32)]
  transfers between devices with their start and end apart: 46 -> 37, of which waited for: 21 -> 18; matrix products, arithmetic and copies ran while one was open for 24% -> 31% of each run, Pallas kernels for 0% -> 0%
where the time goes in v2:
time: 540 us; the launch traced here: 535 us
  waiting for transfers between devices  168 us (31%)
  local copies, waits for them, and re-layouts  116 us (21%)
  matrix products  106 us (20%)
  other arithmetic  82.9 us (15%)
  between operations  31.2 us (6%)
  starting transfers between devices  30.1 us (6%)
    ppermute x25, waiting for transfers between devices, step(): self.state = kept + lax.ppermute(given, place[0], swap_pairs(*place))  86.9 us
    ppermute x5, waiting for transfers between devices, gather_rows(): other = lax.ppermute(piece, place[0], swap_pairs(*place))  70.4 us
    dot_general x7, matrix products, project_back(): lax.dot_general(flat_rows, weight, (((1,), (1,)), ((), ())), preferred_el...  30 us
    dot_general x7, matrix products, project(): jnp.dot(flat_rows, weight, preferred_element_type=jnp.float32)  28.8 us
    convert_element_type x1, other arithmetic, shards(): hidden = gelu_exact(gate_rows).astype(jnp.bfloat16)  26.2 us
    unnamed x143, local copies, waits for them, and re-layouts  21.4 us
    dot_general x7, matrix products, weight_grad(): lax.dot_general(left_rows.reshape(-1, left_rows.shape[-1]), right_rows.re...  19.9 us
    ppermute x25, starting transfers between devices, step(): self.state = kept + lax.ppermute(given, place[0], swap_pairs(*place))  18.5 us
  transfers between devices with their start and end apart: 37, of which 18 were waited for; matrix products, arithmetic and copies ran while one was open for 31% of the time, Pallas kernels for 0%

profile of v2, /device:TPU:0, one launch (start us, length us, event | category | flops | bytes accessed | tf_op | source)
XLA Modules:
  0.0 534.8 jit_solution(16048621756405253909)
XLA Ops:
  44.6 19.9 %collective-permute-done.1 = bf16[1,2,1,1,1,24,2432]{6,5,4,3,2,1,0:T(8,128)(2,1)S(1)} collective-permute-done((bf16[1,2,1,1,1,24,2432]{6,5,4,3,2,1,0:T(8,128)(2,1)S(1)}, bf16[1,2,1,1,1,24,2432]{6,5,4,3,2,1,0:T(8,128)(2,1)S(1)}, u32[]{:S(2)}, u32[]{:S(2)}) %collective-permute-start.1) | collective-permute-done | bytes 233504 | tf_op jit(solution)/shard_map/ppermute | solution.py:206
  69.3 9.6 %collective-permute-done.2 = bf16[2,2,1,1,1,24,2432]{6,5,4,3,2,1,0:T(8,128)(2,1)S(1)} collective-permute-done((bf16[2,2,1,1,1,24,2432]{6,5,4,3,2,1,0:T(8,128)(2,1)S(1)}, bf16[2,2,1,1,1,24,2432]{6,5,4,3,2,1,0:T(8,128)(2,1)S(1)}, u32[]{:S(2)}, u32[]{:S(2)}) %collective-permute-start.2) | collective-permute-done | bytes 466976 | tf_op jit(solution)/shard_map/ppermute | solution.py:206
  84.4 40.9 %collective-permute-done.3 = bf16[2,2,2,1,1,24,2432]{6,5,4,3,2,1,0:T(8,128)(2,1)S(1)} collective-permute-done((bf16[2,2,2,1,1,24,2432]{6,5,4,3,2,1,0:T(8,128)(2,1)}, bf16[2,2,2,1,1,24,2432]{6,5,4,3,2,1,0:T(8,128)(2,1)S(1)}, u32[]{:S(2)}, u32[]{:S(2)}) %collective-permute-start.3) | collective-permute-done | bytes 933920 | tf_op jit(solution)/shard_map/ppermute | solution.py:206
  147.7 4.2 convolution_convert_fusion
  160.7 4.2 convolution_convert_fusion.1
  180.7 4.7 slice.178
  185.5 9.8 %reshape.438 = bf16[32,24,4,768]{3,2,1,0:T(4,128)(2,1)} reshape(bf16[768,3072]{1,0:T(8,128)(2,1)} %slice.178) | data formatting | bytes 9437184 | tf_op jit(solution)/shard_map/reshape | solution.py:314
  195.2 5.5 %copy.168 = bf16[32,4,24,768]{3,2,1,0:T(8,128)(2,1)} copy(bf16[32,4,24,768]{3,1,2,0:T(4,128)(2,1)} %bitcast.219) | data formatting | bytes 9437184 | tf_op jit(solution)/shard_map/transpose | solution.py:315
  209.0 6.6 %fusion.45 = (u8[128,3072]{1,0:T(8,128)(4,1)S(1)}, u8[128,3072]{1,0:T(8,128)(4,1)S(1)}, f32[4,128,3072]{2,1,0:T(8,128)S(1)}) fusion(bf16[768,9984]{1,0:T(8,128)(2,1)} %all-gather.2.cloned.1.call-done, f32[4,128,768]{2,1,0:T(8,128)S(1)} %subtract_multiply_fusion, f32[768]{0:T(1024)S(1)} %get-tuple-element.129, f32[768]{0:T(1024)S(1)} %get-tuple-element.128), kind=kOutput, calls=%fused_computation.117 | convolution fusion | flops 2436759552 | bytes 13375488 | tf_op jit(solution)/shard_map/dot_general | solution.py:21
  215.6 26.2 %multiply_convert_fusion = (bf16[4,128,3072]{2,1,0:T(8,128)(2,1)S(1)}, f32[4,128,3072]{2,1,0:T(8,128)S(1)}) fusion(f32[4,128,3072]{2,1,0:T(8,128)S(1)} %get-tuple-element.176, u8[128,3072]{1,0:T(8,128)(4,1)S(1)} %get-tuple-element.118, u8[128,3072]{1,0:T(8,128)(4,1)S(1)} %get-tuple-element.117), kind=kLoop, calls=%fused_computation.16 | loop fusion | flops 110100480 | bytes 16515072 | tf_op jit(solution)/shard_map/convert_element_type | solution.py:345
  248.1 7.7 %add_convert_fusion = bf16[4,128,3072]{2,1,0:T(8,128)(2,1)} fusion(f32[4,128,3072]{2,1,0:T(8,128)S(1)} %get-tuple-element.135, f32[4,128,3072]{2,1,0:T(8,128)S(1)} %get-tuple-element.176, bf16[4,128,768]{2,1,0:T(8,128)(2,1)S(1)} %copy-done.45, bf16[3072,768,1]{1,0,2:T(8,128)(2,1)} %bitcast.249), kind=kOutput, calls=%fused_computation.15 | convolution fusion | flops 2437939200 | bytes 21233664 | tf_op jit(solution)/shard_map/dot_general | solution.py:28
  255.9 5.2 bitcast_convert_fusion
  261.1 6.0 %select_convert_fusion = bf16[4,128,768]{2,1,0:T(8,128)(2,1)} fusion(f32[4,128,768]{2,1,0:T(8,128)S(1)} %get-tuple-element.175, bf16[4,128,3072]{2,1,0:T(8,128)(2,1)S(1)} %copy-done.36, bf16[3072,768,1]{1,0,2:T(8,128)(2,1)} %bitcast.250, pred[4,128]{1,0:T(4,128)(4,1)S(1)} %iota_compare_fusion.2), kind=kOutput, calls=%fused_computation.109 | convolution fusion | flops 2417098752 | bytes 10224128 | tf_op jit(solution)/shard_map/dot_general | solution.py:21
  271.4 5.1 fusion.76
  284.2 20.4 %collective-permute-done.9 = bf16[2,2,1,2,1,96,768]{6,5,4,3,2,1,0:T(8,128)(2,1)S(1)} collective-permute-done((bf16[2,2,1,2,1,96,768]{6,5,4,3,2,1,0:T(8,128)(2,1)S(1)}, bf16[2,2,1,2,1,96,768]{6,5,4,3,2,1,0:T(8,128)(2,1)S(1)}, u32[]{:S(2)}, u32[]{:S(2)}) %collective-permute-start.9) | collective-permute-done | bytes 1179680 | tf_op jit(solution)/shard_map/ppermute | solution.py:228
  312.3 4.5 multiply_reduce_fusion
  324.8 4.8 multiply_convert_fusion.3
  346.7 3.4 fusion.38
  359.4 3.8 fusion.47
  368.5 4.3 collective-permute-done.19
  372.7 6.9 %collective-permute-done.18 = bf16[1,196,768]{2,1,0:T(8,128)(2,1)S(1)} collective-permute-done((bf16[1,196,768]{2,1,0:T(8,128)(2,1)S(1)}, bf16[1,196,768]{2,1,0:T(8,128)(2,1)S(1)}, u32[]{:S(2)}, u32[]{:S(2)}) %collective-permute-start.18) | collective-permute-done | bytes 301088 | tf_op jit(solution)/shard_map/ppermute | solution.py:250
  402.5 3.7 constant_dynamic-slice_fusion.20
  426.5 4.0 bitcast_convert_fusion.2
  430.5 4.0 fusion.14
  452.2 9.2 %collective-permute-done.26 = bf16[2,2,2,1,1,24,1152]{6,5,4,3,2,1,0:T(8,128)(2,1)S(1)} collective-permute-done((bf16[2,2,2,1,1,24,1152]{6,5,4,3,2,1,0:T(8,128)(2,1)S(1)}, bf16[2,2,2,1,1,24,1152]{6,5,4,3,2,1,0:T(8,128)(2,1)S(1)}, u32[]{:S(2)}, u32[]{:S(2)}) %collective-permute-start.26) | collective-permute-done | bytes 442400 | tf_op jit(solution)/shard_map/ppermute | solution.py:228
  463.1 10.2 %collective-permute-done.30 = bf16[2,2,1,2,1,24,3840]{6,5,4,3,2,1,0:T(8,128)(2,1)} collective-permute-done((bf16[2,2,1,2,1,24,3840]{6,5,4,3,2,1,0:T(8,128)(2,1)}, bf16[2,2,1,2,1,24,3840]{6,5,4,3,2,1,0:T(8,128)(2,1)}, u32[]{:S(2)}, u32[]{:S(2)}) %collective-permute-start.30) | collective-permute-done | bytes 1474592 | tf_op jit(solution)/shard_map/ppermute | solution.py:228
  475.7 8.1 %collective-permute-done.21 = bf16[2,2,1,2,1,24,1280]{6,5,4,3,2,1,0:T(8,128)(2,1)S(1)} collective-permute-done((bf16[2,2,1,2,1,24,1280]{6,5,4,3,2,1,0:T(8,128)(2,1)S(1)}, bf16[2,2,1,2,1,24,1280]{6,5,4,3,2,1,0:T(8,128)(2,1)S(1)}, u32[]{:S(2)}, u32[]{:S(2)}) %collective-permute-start.21) | collective-permute-done | bytes 491552 | tf_op jit(solution)/shard_map/ppermute | solution.py:228
  483.9 3.7 collective-permute-done.27
  489.0 6.0 %collective-permute-done.28 = bf16[1,2,1,1,1,24,1152]{6,5,4,3,2,1,0:T(8,128)(2,1)S(1)} collective-permute-done((bf16[1,2,1,1,1,24,1152]{6,5,4,3,2,1,0:T(8,128)(2,1)S(1)}, bf16[1,2,1,1,1,24,1152]{6,5,4,3,2,1,0:T(8,128)(2,1)S(1)}, u32[]{:S(2)}, u32[]{:S(2)}) %collective-permute-start.28) | collective-permute-done | bytes 110624 | tf_op jit(solution)/shard_map/ppermute | solution.py:228
  500.2 3.9 collective-permute-done.23
  510.0 10.6 %collective-permute-done.32 = bf16[1,2,1,1,1,24,3840]{6,5,4,3,2,1,0:T(8,128)(2,1)S(1)} collective-permute-done((bf16[1,2,1,1,1,24,3840]{6,5,4,3,2,1,0:T(8,128)(2,1)S(1)}, bf16[1,2,1,1,1,24,3840]{6,5,4,3,2,1,0:T(8,128)(2,1)S(1)}, u32[]{:S(2)}, u32[]{:S(2)}) %collective-permute-start.32) | collective-permute-done | bytes 368672 | tf_op jit(solution)/shard_map/ppermute | solution.py:228
  521.5 4.8 collective-permute-done.33
  (400 shorter events, 231.8 us)
Async XLA Ops:
  7.2 153.5 %all-gather.2.cloned.1.call-start = ((), (), s32[]{:S(2)}) async-start(), calls=%async_computation | async-start | bytes 15814656 | tf_op jit(solution)/shard_map/all_gather | solution.py:294
  17.1 22.0 %collective-permute-start = (bf16[1,1,1,1,1,24,2432]{6,5,4,3,2,1,0:T(8,128)(2,1)S(1)}, bf16[1,1,1,1,1,24,2432]{6,5,4,3,2,1,0:T(8,128)(2,1)S(1)}, u32[]{:S(2)}, u32[]{:S(2)}) collective-permute-start(bf16[1,1,1,1,1,24,2432]{6,5,4,3,2,1,0:T(8,128)(2,1)S(1)} %fusion.66), channel_id=1, source_target_pairs={{0,8},{4,12},{8,0},{12,4},{16,24},{20,28},{24,16},{28,20},{1,9},{5... | collective-permute-start | bytes 350216 | tf_op jit(solution)/shard_map/ppermute | solution.py:206
  33.8 105.3 %collective-permute-start.7 = (bf16[1,196,768]{2,1,0:T(8,128)(2,1)S(1)}, bf16[1,196,768]{2,1,0:T(8,128)(2,1)}, u32[]{:S(2)}, u32[]{:S(2)}) collective-permute-start(bf16[1,196,768]{2,1,0:T(8,128)(2,1)S(1)} %copy_select_fusion), channel_id=1, source_target_pairs={{0,3},{1,2},{2,1},{3,0},{4,7},{5,6},{6,5},{7,4},{8,11},{9,10},{10,... | collective-permute-start | bytes 903176 | tf_op jit(solution)/shard_map/ppermute | solution.py:250
  35.3 103.7 %collective-permute-start.5 = (bf16[1,196,768]{2,1,0:T(8,128)(2,1)}, bf16[1,196,768]{2,1,0:T(8,128)(2,1)}, u32[]{:S(2)}, u32[]{:S(2)}) collective-permute-start(bf16[1,196,768]{2,1,0:T(8,128)(2,1)} %copy_select_fusion.2), channel_id=1, source_target_pairs={{0,1},{1,0},{2,3},{3,2},{4,5},{5,4},{6,7},{7,6},{8,9},{9,8},{10,11... | collective-permute-start | bytes 903176 | tf_op jit(solution)/shard_map/ppermute | solution.py:250
  40.6 23.8 %collective-permute-start.1 = (bf16[1,2,1,1,1,24,2432]{6,5,4,3,2,1,0:T(8,128)(2,1)S(1)}, bf16[1,2,1,1,1,24,2432]{6,5,4,3,2,1,0:T(8,128)(2,1)S(1)}, u32[]{:S(2)}, u32[]{:S(2)}) collective-permute-start(bf16[1,2,1,1,1,24,2432]{6,5,4,3,2,1,0:T(8,128)(2,1)S(1)} %constant_dynamic-slice_fusion.33), channel_id=1, source_target_pairs={{0,16},{4,20},{8,24},{12,28},{16,0},{20,4},{24,8},{28,12},{1,17},{... | collective-permute-start | bytes 700424 | tf_op jit(solution)/shard_map/ppermute | solution.py:206
  44.1 95.0 %collective-permute-start.6 = (bf16[1,196,768]{2,1,0:T(8,128)(2,1)}, bf16[1,196,768]{2,1,0:T(8,128)(2,1)}, u32[]{:S(2)}, u32[]{:S(2)}) collective-permute-start(bf16[1,196,768]{2,1,0:T(8,128)(2,1)} %copy_select_fusion.1), channel_id=1, source_target_pairs={{0,2},{1,3},{2,0},{3,1},{4,6},{5,7},{6,4},{7,5},{8,10},{9,11},{10,... | collective-permute-start | bytes 903176 | tf_op jit(solution)/shard_map/ppermute | solution.py:250
  66.3 12.6 %collective-permute-start.2 = (bf16[2,2,1,1,1,24,2432]{6,5,4,3,2,1,0:T(8,128)(2,1)S(1)}, bf16[2,2,1,1,1,24,2432]{6,5,4,3,2,1,0:T(8,128)(2,1)S(1)}, u32[]{:S(2)}, u32[]{:S(2)}) collective-permute-start(bf16[2,2,1,1,1,24,2432]{6,5,4,3,2,1,0:T(8,128)(2,1)S(1)} %constant_dynamic-slice_fusion.32), channel_id=1, source_target_pairs={{0,4},{4,0},{8,12},{12,8},{16,20},{20,16},{24,28},{28,24},{1,5},{5... | collective-permute-start | bytes 1400840 | tf_op jit(solution)/shard_map/ppermute | solution.py:206
  82.2 43.1 %collective-permute-start.3 = (bf16[2,2,2,1,1,24,2432]{6,5,4,3,2,1,0:T(8,128)(2,1)}, bf16[2,2,2,1,1,24,2432]{6,5,4,3,2,1,0:T(8,128)(2,1)S(1)}, u32[]{:S(2)}, u32[]{:S(2)}) collective-permute-start(bf16[2,2,2,1,1,24,2432]{6,5,4,3,2,1,0:T(8,128)(2,1)} %constant_dynamic-slice_fusion.31), channel_id=1, source_target_pairs={{0,2},{1,3},{2,0},{3,1},{4,6},{5,7},{6,4},{7,5},{8,10},{9,11},{10,... | collective-permute-start | bytes 2801672 | tf_op jit(solution)/shard_map/ppermute | solution.py:206
  129.3 12.8 %collective-permute-start.4 = (bf16[2,2,2,2,1,24,2432]{6,5,4,3,2,1,0:T(8,128)(2,1)}, bf16[2,2,2,2,1,24,2432]{6,5,4,3,2,1,0:T(8,128)(2,1)}, u32[]{:S(2)}, u32[]{:S(2)}) collective-permute-start(bf16[2,2,2,2,1,24,2432]{6,5,4,3,2,1,0:T(8,128)(2,1)} %constant_dynamic-slice_fusion.30), channel_id=1, source_target_pairs={{0,1},{1,0},{2,3},{3,2},{4,5},{5,4},{6,7},{7,6},{8,9},{9,8},{10,11... | collective-permute-start | bytes 5603336 | tf_op jit(solution)/shard_map/ppermute | solution.py:206
  247.6 19.5 %collective-permute-start.8 = (bf16[2,2,2,2,1,96,768]{6,5,4,3,2,1,0:T(8,128)(2,1)}, bf16[2,2,2,2,1,96,768]{6,5,4,3,2,1,0:T(8,128)(2,1)}, u32[]{:S(2)}, u32[]{:S(2)}) collective-permute-start(bf16[2,2,2,2,1,96,768]{6,5,4,3,2,1,0:T(8,128)(2,1)} %constant_dynamic-slice_fusion.28), channel_id=1, source_target_pairs={{0,1},{1,0},{2,3},{3,2},{4,5},{5,4},{6,7},{7,6},{8,9},{9,8},{10,11... | collective-permute-start | bytes 7077896 | tf_op jit(solution)/shard_map/ppermute | solution.py:228
  269.3 36.4 %collective-permute-start.10 = (bf16[2,2,2,2,1,24,3072]{6,5,4,3,2,1,0:T(8,128)(2,1)S(1)}, bf16[2,2,2,2,1,24,3072]{6,5,4,3,2,1,0:T(8,128)(2,1)S(1)}, u32[]{:S(2)}, u32[]{:S(2)}) collective-permute-start(bf16[2,2,2,2,1,24,3072]{6,5,4,3,2,1,0:T(8,128)(2,1)S(1)} %constant_dynamic-slice_fusion.26), channel_id=1, source_target_pairs={{0,1},{1,0},{2,3},{3,2},{4,5},{5,4},{6,7},{7,6},{8,9},{9,8},{10,11... | collective-permute-start | bytes 7077896 | tf_op jit(solution)/shard_map/ppermute | solution.py:228
  276.6 27.9 %collective-permute-start.9 = (bf16[2,2,1,2,1,96,768]{6,5,4,3,2,1,0:T(8,128)(2,1)S(1)}, bf16[2,2,1,2,1,96,768]{6,5,4,3,2,1,0:T(8,128)(2,1)S(1)}, u32[]{:S(2)}, u32[]{:S(2)}) collective-permute-start(bf16[2,2,1,2,1,96,768]{6,5,4,3,2,1,0:T(8,128)(2,1)S(1)} %constant_dynamic-slice_fusion.27), channel_id=1, source_target_pairs={{0,4},{4,0},{8,12},{12,8},{16,20},{20,16},{24,28},{28,24},{1,5},{5... | collective-permute-start | bytes 3538952 | tf_op jit(solution)/shard_map/ppermute | solution.py:228
  312.2 27.3 %collective-permute-start.11 = (bf16[2,2,2,1,1,24,3072]{6,5,4,3,2,1,0:T(8,128)(2,1)}, bf16[2,2,2,1,1,24,3072]{6,5,4,3,2,1,0:T(8,128)(2,1)}, u32[]{:S(2)}, u32[]{:S(2)}) collective-permute-start(bf16[2,2,2,1,1,24,3072]{6,5,4,3,2,1,0:T(8,128)(2,1)} %constant_dynamic-slice_fusion.25), channel_id=1, source_target_pairs={{0,2},{1,3},{2,0},{3,1},{4,6},{5,7},{6,4},{7,5},{8,10},{9,11},{10,... | collective-permute-start | bytes 3538952 | tf_op jit(solution)/shard_map/ppermute | solution.py:228
  342.7 44.2 %collective-permute-start.13 = (bf16[2,2,1,1,1,24,3072]{6,5,4,3,2,1,0:T(8,128)(2,1)}, bf16[2,2,1,1,1,24,3072]{6,5,4,3,2,1,0:T(8,128)(2,1)}, u32[]{:S(2)}, u32[]{:S(2)}) collective-permute-start(bf16[2,2,1,1,1,24,3072]{6,5,4,3,2,1,0:T(8,128)(2,1)} %constant_dynamic-slice_fusion.23), channel_id=1, source_target_pairs={{0,4},{4,0},{8,12},{12,8},{16,20},{20,16},{24,28},{28,24},{1,5},{5... | collective-permute-start | bytes 1769480 | tf_op jit(solution)/shard_map/ppermute | solution.py:228
  344.3 44.7 %collective-permute-start.12 = (bf16[2,2,1,1,1,96,768]{6,5,4,3,2,1,0:T(8,128)(2,1)}, bf16[2,2,1,1,1,96,768]{6,5,4,3,2,1,0:T(8,128)(2,1)}, u32[]{:S(2)}, u32[]{:S(2)}) collective-permute-start(bf16[2,2,1,1,1,96,768]{6,5,4,3,2,1,0:T(8,128)(2,1)} %constant_dynamic-slice_fusion.24), channel_id=1, source_target_pairs={{0,2},{1,3},{2,0},{3,1},{4,6},{5,7},{6,4},{7,5},{8,10},{9,11},{10,... | collective-permute-start | bytes 1769480 | tf_op jit(solution)/shard_map/ppermute | solution.py:228
  363.4 9.3 %collective-permute-start.19 = (bf16[1,196,768]{2,1,0:T(8,128)(2,1)S(1)}, bf16[1,196,768]{2,1,0:T(8,128)(2,1)S(1)}, u32[]{:S(2)}, u32[]{:S(2)}) collective-permute-start(bf16[1,196,768]{2,1,0:T(8,128)(2,1)S(1)} %get-tuple-element.144), channel_id=1, source_target_pairs={{0,3},{1,2},{2,1},{3,0},{4,7},{5,6},{6,5},{7,4},{8,11},{9,10},{10,... | collective-permute-start | bytes 903176 | tf_op jit(solution)/shard_map/ppermute | solution.py:250
  363.5 16.1 %collective-permute-start.18 = (bf16[1,196,768]{2,1,0:T(8,128)(2,1)S(1)}, bf16[1,196,768]{2,1,0:T(8,128)(2,1)S(1)}, u32[]{:S(2)}, u32[]{:S(2)}) collective-permute-start(bf16[1,196,768]{2,1,0:T(8,128)(2,1)S(1)} %get-tuple-element.145), channel_id=1, source_target_pairs={{0,2},{1,3},{2,0},{3,1},{4,6},{5,7},{6,4},{7,5},{8,10},{9,11},{10,... | collective-permute-start | bytes 903176 | tf_op jit(solution)/shard_map/ppermute | solution.py:250
  365.3 14.3 %collective-permute-start.17 = (bf16[1,196,768]{2,1,0:T(8,128)(2,1)S(1)}, bf16[1,196,768]{2,1,0:T(8,128)(2,1)S(1)}, u32[]{:S(2)}, u32[]{:S(2)}) collective-permute-start(bf16[1,196,768]{2,1,0:T(8,128)(2,1)S(1)} %get-tuple-element.146), channel_id=1, source_target_pairs={{0,1},{1,0},{2,3},{3,2},{4,5},{5,4},{6,7},{7,6},{8,9},{9,8},{10,11... | collective-permute-start | bytes 903176 | tf_op jit(solution)/shard_map/ppermute | solution.py:250
  399.6 23.6 %collective-permute-start.15 = (bf16[1,2,1,1,1,24,3072]{6,5,4,3,2,1,0:T(8,128)(2,1)}, bf16[1,2,1,1,1,24,3072]{6,5,4,3,2,1,0:T(8,128)(2,1)S(1)}, u32[]{:S(2)}, u32[]{:S(2)}) collective-permute-start(bf16[1,2,1,1,1,24,3072]{6,5,4,3,2,1,0:T(8,128)(2,1)} %constant_dynamic-slice_fusion.21), channel_id=1, source_target_pairs={{0,16},{4,20},{8,24},{12,28},{16,0},{20,4},{24,8},{28,12},{1,17},{... | collective-permute-start | bytes 884744 | tf_op jit(solution)/shard_map/ppermute | solution.py:228
  399.6 22.6 %collective-permute-start.14 = (bf16[1,2,1,1,1,96,768]{6,5,4,3,2,1,0:T(8,128)(2,1)}, bf16[1,2,1,1,1,96,768]{6,5,4,3,2,1,0:T(8,128)(2,1)}, u32[]{:S(2)}, u32[]{:S(2)}) collective-permute-start(bf16[1,2,1,1,1,96,768]{6,5,4,3,2,1,0:T(8,128)(2,1)} %constant_dynamic-slice_fusion.22), channel_id=1, source_target_pairs={{0,16},{4,20},{8,24},{12,28},{16,0},{20,4},{24,8},{28,12},{1,17},{... | collective-permute-start | bytes 884744 | tf_op jit(solution)/shard_map/ppermute | solution.py:228
  406.2 17.1 %collective-permute-start.16 = (bf16[2,2,2,2,1,24,3840]{6,5,4,3,2,1,0:T(8,128)(2,1)}, bf16[2,2,2,2,1,24,3840]{6,5,4,3,2,1,0:T(8,128)(2,1)}, u32[]{:S(2)}, u32[]{:S(2)}) collective-permute-start(bf16[2,2,2,2,1,24,3840]{6,5,4,3,2,1,0:T(8,128)(2,1)} %constant_dynamic-slice_fusion.20), channel_id=1, source_target_pairs={{0,1},{1,0},{2,3},{3,2},{4,5},{5,4},{6,7},{7,6},{8,9},{9,8},{10,11... | collective-permute-start | bytes 8847368 | tf_op jit(solution)/shard_map/ppermute | solution.py:228
  434.6 13.2 %collective-permute-start.35 = (bf16[1,1,1,1,1,96,768]{6,5,4,3,2,1,0:T(8,128)(2,1)S(1)}, bf16[1,1,1,1,1,96,768]{6,5,4,3,2,1,0:T(8,128)(2,1)}, u32[]{:S(2)}, u32[]{:S(2)}) collective-permute-start(bf16[1,1,1,1,1,96,768]{6,5,4,3,2,1,0:T(8,128)(2,1)S(1)} %constant_dynamic-slice_fusion.4), channel_id=1, source_target_pairs={{0,8},{4,12},{8,0},{12,4},{16,24},{20,28},{24,16},{28,20},{1,9},{5... | collective-permute-start | bytes 442376 | tf_op jit(solution)/shard_map/ppermute | solution.py:228
  434.7 11.5 %collective-permute-start.34 = (bf16[1,1,1,1,1,24,3072]{6,5,4,3,2,1,0:T(8,128)(2,1)S(1)}, bf16[1,1,1,1,1,24,3072]{6,5,4,3,2,1,0:T(8,128)(2,1)}, u32[]{:S(2)}, u32[]{:S(2)}) collective-permute-start(bf16[1,1,1,1,1,24,3072]{6,5,4,3,2,1,0:T(8,128)(2,1)S(1)} %constant_dynamic-slice_fusion.5), channel_id=1, source_target_pairs={{0,8},{4,12},{8,0},{12,4},{16,24},{20,28},{24,16},{28,20},{1,9},{5... | collective-permute-start | bytes 442376 | tf_op jit(solution)/shard_map/ppermute | solution.py:228
  437.9 35.5 %collective-permute-start.30 = (bf16[2,2,1,2,1,24,3840]{6,5,4,3,2,1,0:T(8,128)(2,1)}, bf16[2,2,1,2,1,24,3840]{6,5,4,3,2,1,0:T(8,128)(2,1)}, u32[]{:S(2)}, u32[]{:S(2)}) collective-permute-start(bf16[2,2,1,2,1,24,3840]{6,5,4,3,2,1,0:T(8,128)(2,1)} %constant_dynamic-slice_fusion.9), channel_id=1, source_target_pairs={{0,4},{4,0},{8,12},{12,8},{16,20},{20,16},{24,28},{28,24},{1,5},{5... | collective-permute-start | bytes 4423688 | tf_op jit(solution)/shard_map/ppermute | solution.py:228
  442.5 7.9 %collective-permute-start.20 = (bf16[2,2,2,2,1,24,1280]{6,5,4,3,2,1,0:T(8,128)(2,1)S(1)}, bf16[2,2,2,2,1,24,1280]{6,5,4,3,2,1,0:T(8,128)(2,1)S(1)}, u32[]{:S(2)}, u32[]{:S(2)}) collective-permute-start(bf16[2,2,2,2,1,24,1280]{6,5,4,3,2,1,0:T(8,128)(2,1)S(1)} %fusion.53), channel_id=1, source_target_pairs={{0,1},{1,0},{2,3},{3,2},{4,5},{5,4},{6,7},{7,6},{8,9},{9,8},{10,11... | collective-permute-start | bytes 2949128 | tf_op jit(solution)/shard_map/ppermute | solution.py:228
  449.7 11.8 %collective-permute-start.26 = (bf16[2,2,2,1,1,24,1152]{6,5,4,3,2,1,0:T(8,128)(2,1)S(1)}, bf16[2,2,2,1,1,24,1152]{6,5,4,3,2,1,0:T(8,128)(2,1)S(1)}, u32[]{:S(2)}, u32[]{:S(2)}) collective-permute-start(bf16[2,2,2,1,1,24,1152]{6,5,4,3,2,1,0:T(8,128)(2,1)S(1)} %constant_dynamic-slice_fusion.13), channel_id=1, source_target_pairs={{0,2},{1,3},{2,0},{3,1},{4,6},{5,7},{6,4},{7,5},{8,10},{9,11},{10,... | collective-permute-start | bytes 1327112 | tf_op jit(solution)/shard_map/ppermute | solution.py:228
  450.6 33.2 %collective-permute-start.21 = (bf16[2,2,1,2,1,24,1280]{6,5,4,3,2,1,0:T(8,128)(2,1)S(1)}, bf16[2,2,1,2,1,24,1280]{6,5,4,3,2,1,0:T(8,128)(2,1)S(1)}, u32[]{:S(2)}, u32[]{:S(2)}) collective-permute-start(bf16[2,2,1,2,1,24,1280]{6,5,4,3,2,1,0:T(8,128)(2,1)S(1)} %constant_dynamic-slice_fusion.18), channel_id=1, source_target_pairs={{0,4},{4,0},{8,12},{12,8},{16,20},{20,16},{24,28},{28,24},{1,5},{5... | collective-permute-start | bytes 1474568 | tf_op jit(solution)/shard_map/ppermute | solution.py:228
  461.5 26.0 %collective-permute-start.27 = (bf16[2,2,1,1,1,24,1152]{6,5,4,3,2,1,0:T(8,128)(2,1)S(1)}, bf16[2,2,1,1,1,24,1152]{6,5,4,3,2,1,0:T(8,128)(2,1)S(1)}, u32[]{:S(2)}, u32[]{:S(2)}) collective-permute-start(bf16[2,2,1,1,1,24,1152]{6,5,4,3,2,1,0:T(8,128)(2,1)S(1)} %constant_dynamic-slice_fusion.12), channel_id=1, source_target_pairs={{0,4},{4,0},{8,12},{12,8},{16,20},{20,16},{24,28},{28,24},{1,5},{5... | collective-permute-start | bytes 663560 | tf_op jit(solution)/shard_map/ppermute | solution.py:228
  475.1 29.2 %collective-permute-start.31 = (bf16[2,2,1,1,1,24,3840]{6,5,4,3,2,1,0:T(8,128)(2,1)S(1)}, bf16[2,2,1,1,1,24,3840]{6,5,4,3,2,1,0:T(8,128)(2,1)S(1)}, u32[]{:S(2)}, u32[]{:S(2)}) collective-permute-start(bf16[2,2,1,1,1,24,3840]{6,5,4,3,2,1,0:T(8,128)(2,1)S(1)} %constant_dynamic-slice_fusion.8), channel_id=1, source_target_pairs={{0,2},{1,3},{2,0},{3,1},{4,6},{5,7},{6,4},{7,5},{8,10},{9,11},{10,... | collective-permute-start | bytes 2211848 | tf_op jit(solution)/shard_map/ppermute | solution.py:228
  487.6 7.4 %collective-permute-start.28 = (bf16[1,2,1,1,1,24,1152]{6,5,4,3,2,1,0:T(8,128)(2,1)S(1)}, bf16[1,2,1,1,1,24,1152]{6,5,4,3,2,1,0:T(8,128)(2,1)S(1)}, u32[]{:S(2)}, u32[]{:S(2)}) collective-permute-start(bf16[1,2,1,1,1,24,1152]{6,5,4,3,2,1,0:T(8,128)(2,1)S(1)} %constant_dynamic-slice_fusion.11), channel_id=1, source_target_pairs={{0,16},{4,20},{8,24},{12,28},{16,0},{20,4},{24,8},{28,12},{1,17},{... | collective-permute-start | bytes 331784 | tf_op jit(solution)/shard_map/ppermute | solution.py:228
  487.9 8.9 %collective-permute-start.22 = (bf16[2,2,1,1,1,24,1280]{6,5,4,3,2,1,0:T(8,128)(2,1)S(1)}, bf16[2,2,1,1,1,24,1280]{6,5,4,3,2,1,0:T(8,128)(2,1)S(1)}, u32[]{:S(2)}, u32[]{:S(2)}) collective-permute-start(bf16[2,2,1,1,1,24,1280]{6,5,4,3,2,1,0:T(8,128)(2,1)S(1)} %constant_dynamic-slice_fusion.17), channel_id=1, source_target_pairs={{0,2},{1,3},{2,0},{3,1},{4,6},{5,7},{6,4},{7,5},{8,10},{9,11},{10,... | collective-permute-start | bytes 737288 | tf_op jit(solution)/shard_map/ppermute | solution.py:228
  504.4 16.2 %collective-permute-start.32 = (bf16[1,2,1,1,1,24,3840]{6,5,4,3,2,1,0:T(8,128)(2,1)S(1)}, bf16[1,2,1,1,1,24,3840]{6,5,4,3,2,1,0:T(8,128)(2,1)S(1)}, u32[]{:S(2)}, u32[]{:S(2)}) collective-permute-start(bf16[1,2,1,1,1,24,3840]{6,5,4,3,2,1,0:T(8,128)(2,1)S(1)} %constant_dynamic-slice_fusion.7), channel_id=1, source_target_pairs={{0,16},{4,20},{8,24},{12,28},{16,0},{20,4},{24,8},{28,12},{1,17},{... | collective-permute-start | bytes 1105928 | tf_op jit(solution)/shard_map/ppermute | solution.py:228
  (70 other events, 452.7 us)
Sparse Core Ops, SparseCore 0:
  15.5 130.7 all-gather.1
